TPU v7x, 32 devices: a whole 2x2x4 slice. The times are simulated.
32 devices in a mesh: lat: 4 (over y, core), lon: 8 (over z, x).
Axes of the slice: x: 2, y: 2, z: 4, core: 2. Of those that a mesh axis runs over, the one named last changes fastest.
Arguments:
- control: bfloat16 [80, 32, 64, 512], P(None, None, 'lon', 'lat'), may hold values from -6 to 6
- ensemble: bfloat16 [80, 32, 64, 512], P(None, None, 'lon', 'lat'), may hold values from -1.1953125 to 1.1953125
- level_mix: bfloat16 [32, 32], replicated, may hold values from -1 to 1
- lat_taps: float32 [4], replicated, may hold values from 0.1 to 0.6
- lon_taps: float32 [4], replicated, may hold values from 0.1 to 0.6
- obs_location: int32 [8, 4, 2048], P('lon', 'lat'), may hold values from 0 to 32767
- obs_count: int32 [8, 4], P('lon', 'lat'), may hold values from 512 to 2048, as said below
- obs_keep: int32 [8, 4, 2048], P('lon', 'lat'), may hold values 0 or 1
- innovation: float32 [8, 4, 2048], P('lon', 'lat'), may hold values from -6 to 6
- obs_weight: float32 [8, 4, 2048], P('lon', 'lat'), may hold values from 0.25 to 4
Outputs:
- gradient: float32 [80, 32, 64, 512], P(None, None, 'lon', 'lat')
- upper_factor: float32 [80, 80], replicated
Inputs may be any that keep to these rules, and one draw needn't show every extreme that they name: `obs_count`: live slots of a tile come first; some tile has all 2048 slots live.
All inputs are finite; a program needn't handle non-finite values. No bound on the sum of `obs_keep` on one device may be relied on, other than what follows from the above.
Results may differ from a plain program's by a relative error of at most 0.0028.
Values may be sent and summed in bfloat16 or wider, within the bound.
A program may use at most 128 MiB of HBM per device.

v0:
```python
import jax
import jax.numpy as jnp
from jax import lax
from jax.sharding import PartitionSpec as P

OFFSETS = (-2, -1, 1, 2)


def with_halo(shard, sides, width, wrap):
    for axis, dim in sides:
        size, length = (lax.axis_size(axis), shard.shape[dim])
        up = [(i, (i + 1) % size) for i in range(size if wrap else size - 1)]
        down = [(j, i) for i, j in up]
        last = lax.slice_in_dim(shard, length - width, length, axis=dim)
        leading = lax.slice_in_dim(shard, 0, width, axis=dim)
        before = lax.ppermute(last, axis, up)
        after = lax.ppermute(leading, axis, down)
        shard = jnp.concatenate([before, shard, after], axis=dim)
    return shard


def taps_along(padded, weights, dimension, direction, extent):
    summed = lax.slice_in_dim(padded, 2, 2 + extent, axis=dimension).astype(jnp.float32)
    for position in range(4):
        begin_at = 2 + direction * OFFSETS[position]
        piece = lax.slice_in_dim(padded, begin_at, begin_at + extent, axis=dimension)
        summed = summed + weights[position] * piece.astype(jnp.float32)
    return summed


def shards(
    control,
    ensemble,
    level_mix,
    lat_taps,
    lon_taps,
    obs_location,
    obs_count,
    obs_keep,
    innovation,
    obs_weight,
):
    members, levels, lon_cells, lat_cells = control.shape
    mixed_levels = jnp.einsum(
        "kl,mlab->mkab", level_mix, control, preferred_element_type=jnp.float32
    ).astype(jnp.bfloat16)
    padded = with_halo(mixed_levels, (("lat", 3),), 2, False)
    rowwise = taps_along(padded, lat_taps, 3, 1, lat_cells)
    widened = with_halo(rowwise, (("lon", 2),), 2, True)
    localized = taps_along(widened, lon_taps, 2, 1, lon_cells)
    increment = jnp.sum(ensemble.astype(jnp.float32) * localized, axis=0)
    places = obs_location[0, 0]
    slot_ids = jnp.arange(places.shape[0], dtype=jnp.int32)
    live_slots = (slot_ids < obs_count[0, 0]).astype(jnp.float32) * obs_keep[0, 0].astype(
        jnp.float32
    )
    weights = live_slots * obs_weight[0, 0]
    flat_inc = increment.reshape(-1)
    misfit = weights * (flat_inc[places] - innovation[0, 0])
    pulled = jnp.zeros_like(flat_inc).at[places].add(misfit).reshape(increment.shape)
    pulled_members = (ensemble.astype(jnp.float32) * pulled[None]).astype(jnp.bfloat16)
    padded_back = with_halo(pulled_members, (("lon", 2),), 2, True)
    colwise = taps_along(padded_back, lon_taps, 2, -1, lon_cells)
    tall_block = with_halo(colwise, (("lat", 3),), 2, False)
    spread = taps_along(tall_block, lat_taps, 3, -1, lat_cells)
    mixed_back = jnp.einsum(
        "kl,mkab->mlab", level_mix, spread.astype(jnp.bfloat16), preferred_element_type=jnp.float32
    )
    gradient = control.astype(jnp.float32) + mixed_back
    columns = ensemble.reshape(members, -1)[:, places]
    scaled = columns.astype(jnp.float32) * jnp.sqrt(weights)[None, :]
    local_gram = jnp.dot(scaled, scaled.T, precision=lax.Precision.HIGHEST)
    tiles_all = lax.axis_size("lat") * lax.axis_size("lon")
    total_obs = places.shape[0] * tiles_all
    identity = jnp.eye(members, dtype=jnp.float32)
    summed_gram = lax.psum(local_gram, ("lat", "lon"))
    upper_factor = jnp.linalg.cholesky(identity + members / total_obs * summed_gram).T
    return (gradient, upper_factor)


def solution(mesh):
    in_specs = (
        P(None, None, "lon", "lat"),
        P(None, None, "lon", "lat"),
        P(),
        P(),
        P(),
        P("lon", "lat", None),
        P("lon", "lat"),
        P("lon", "lat", None),
        P("lon", "lat", None),
        P("lon", "lat", None),
    )
    out_specs = (P(None, None, "lon", "lat"), P())
    return jax.shard_map(shards, mesh=mesh, in_specs=in_specs, out_specs=out_specs, check_vma=False)
```

profile of v0, /device:TPU:1, one launch (start us, length us, event | category | flops | bytes accessed | tf_op | source)
XLA Modules:
  0.0 486.9 jit_solution(9345131680365541441)
XLA Ops:
  1.3 6.3 %convert_bitcast_fusion = bf16[80,32,8,128]{3,1,2,0:T(8,128)(2,1)} fusion(bf16[80,32,8,128]{3,2,1,0:T(8,128)(2,1)} %param.10, bf16[32,32]{1,0:T(8,128)(2,1)S(1)} %copy-done), kind=kOutput, calls=%fused_computation.59 | convolution fusion | flops 170393600 | bytes 10487808 | tf_op jit(solution)/shard_map/kl,mlab->mkab/dot_general | solution.py:44
  7.7 11.1 %fusion.49 = (bf16[80,32,8,2]{3,1,2,0:T(8,128)(2,1)}, bf16[80,32,8,2]{3,1,2,0:T(8,128)(2,1)}) fusion(bf16[80,32,8,128]{3,1,2,0:T(8,128)(2,1)} %convert_bitcast_fusion), kind=kLoop, calls=%fused_computation.90 | loop fusion | bytes 327680 | tf_op jit(solution)/shard_map/slice | solution.py:14
  18.8 7.6 %copy.57 = bf16[80,32,8,2]{0,2,3,1:T(8,128)(2,1)S(1)} copy(bf16[80,32,8,2]{3,1,2,0:T(8,128)(2,1)} %get-tuple-element.17) | data formatting | bytes 163840 | tf_op jit(solution)/shard_map/slice | solution.py:15
  28.3 7.5 %copy.55 = bf16[80,32,8,2]{0,2,3,1:T(8,128)(2,1)S(1)} copy(bf16[80,32,8,2]{3,1,2,0:T(8,128)(2,1)} %get-tuple-element.16) | data formatting | bytes 163840 | tf_op jit(solution)/shard_map/slice | solution.py:14
  35.9 5.0 %collective-permute-start = (bf16[80,32,8,2]{0,2,3,1:T(8,128)(2,1)S(1)}, bf16[80,32,8,2]{0,2,3,1:T(8,128)(2,1)S(1)}, u32[]{:S(2)}, u32[]{:S(2)}) collective-permute-start(bf16[80,32,8,2]{0,2,3,1:T(8,128)(2,1)S(1)} %copy.55), channel_id=1, source_target_pairs={{0,8},{8,16},{16,24},{1,9},{9,17},{17,25},{2,10},{10,18},{18,26},{... | collective-permute-start | bytes 245768 | tf_op jit(solution)/shard_map/ppermute | solution.py:16
  41.5 9.3 %copy.58 = bf16[80,32,8,2]{3,1,2,0:T(8,128)(2,1)} copy(bf16[80,32,8,2]{0,2,3,1:T(8,128)(2,1)S(1)} %collective-permute-done.1) | data formatting | bytes 163840 | tf_op jit(solution)/shard_map/ppermute | solution.py:17
  50.8 9.3 %copy.56 = bf16[80,32,8,2]{3,1,2,0:T(8,128)(2,1)} copy(bf16[80,32,8,2]{0,2,3,1:T(8,128)(2,1)S(1)} %collective-permute-done) | data formatting | bytes 163840 | tf_op jit(solution)/shard_map/ppermute | solution.py:16
  60.1 30.0 %multiply_add_fusion.1 = f32[80,32,8,128]{3,1,2,0:T(8,128)S(1)} fusion(bf16[80,32,8,128]{3,1,2,0:T(8,128)(2,1)} %convert_bitcast_fusion, bf16[80,32,8,2]{3,1,2,0:T(8,128)(2,1)} %copy.58, bf16[80,32,8,2]{3,1,2,0:T(8,128)(2,1)} %copy.56, f32[]{:T(128)} %bitcast.11, f32[]{:T(128)} %bitcast.10, f32[]{:T(128)} %bitcast.9, f32[]{:T(128)} %bitcast.8), kind=kLoop, calls=%fused_computation.46 | loop fusion | flops 65536000 | bytes 15892496 | tf_op jit(solution)/shard_map/add | solution.py:27
  90.8 4.3 collective-permute-start.3
  96.5 108.5 %collective-permute-done.3 = f32[80,32,2,128]{3,1,2,0:T(8,128)S(1)} collective-permute-done((f32[80,32,2,128]{3,1,2,0:T(8,128)S(1)}, f32[80,32,2,128]{3,1,2,0:T(8,128)S(1)}, u32[]{:S(2)}, u32[]{:S(2)}) %collective-permute-start.3) | collective-permute-done | bytes 2621472 | tf_op jit(solution)/shard_map/ppermute | solution.py:17
  207.2 11.6 %fusion = f32[32,8,128]{2,0,1:T(8,128)S(1)} fusion(f32[80,32,8,128]{3,1,2,0:T(8,128)S(1)} %multiply_add_fusion.1, f32[80,32,2,128]{3,1,2,0:T(8,128)S(1)} %collective-permute-done.3, f32[80,32,2,128]{3,1,2,0:T(8,128)} %copy-done.3, f32[]{:T(128)} %bitcast.15, f32[]{:T(128)} %bitcast.14, f32[]{:T(128)} %bitcast.13, f32[]{:T(128)} %bitcast.12, ...), kind=kLoop, calls=%fused_computation.13 | loop fusion | flops 39288832 | bytes 21102608 | tf_op jit(solution)/shard_map/reduce_sum | solution.py:51
  218.9 11.8 %gather_fusion = f32[2048]{0:T(1024)S(1)} fusion(f32[32768]{0:T(1024)S(1)} %bitcast.39, s32[2048]{0:T(1024)S(1)} %broadcast_clamp_fusion), kind=kCustom, calls=%fused_computation | custom fusion | bytes 24576 | tf_op jit(solution)/shard_map/gather | solution.py:59
  230.7 11.5 %scatter_custom_fusion = f32[32768]{0:T(1024)S(1)} fusion(s32[2048]{0:T(1024)S(1)} %bitcast.44, f32[2048]{0:T(1024)S(1)} %get-tuple-element.19, f32[]{:T(128)} %constant.39.clone.1), kind=kCustom, calls=%fused_computation.68 | custom fusion | flops 2048 | bytes 131076 | tf_op jit(solution)/shard_map/scatter-add | solution.py:60
  242.2 4.3 fusion.1
  246.5 2.3 copy-done.2
  248.8 2.0 fusion.48
  250.8 2.2 collective-permute-start.5
  253.0 2.5 collective-permute-start.4
  255.5 10.6 %copy.66 = bf16[80,32,8,128]{0,3,2,1:T(8,128)(2,1)} copy(bf16[80,32,8,128]{3,2,1,0:T(8,128)(2,1)} %param.11) | data formatting | bytes 10485760 | tf_op args[1]
  266.1 10.0 %gather_fusion.1 = bf16[2048,80]{1,0:T(8,128)(2,1)S(1)} fusion(bf16[80,32768]{0,1:T(8,128)(2,1)} %bitcast.40, s32[2048]{0:T(1024)S(1)} %broadcast_clamp_fusion), kind=kCustom, calls=%fused_computation.1 | custom fusion | bytes 663552 | tf_op jit(solution)/shard_map/gather | solution.py:70
  276.1 2.4 fusion.35
  278.5 65.3 %psum.7 = f32[80,80]{0,1:T(8,128)S(1)} all-reduce(f32[80,80]{0,1:T(8,128)S(1)} %fusion.35), channel_id=1, replica_groups=mesh['lat'=4,'lon'=8] {'lat','lon'}, use_global_device_ids=true, to_apply=%region_2.0 | all-reduce | flops 6400 | bytes 51200 | tf_op jit(solution)/shard_map/psum | solution.py:76
  343.9 7.3 %cholesky.20 = f32[80,80]{1,0:T(8,128)S(1)} custom-call(f32[80,80]{1,0:T(8,128)S(1)} %fusion.41), custom_call_target="Cholesky" | custom-call | tf_op jit(solution)/shard_map/jit(cholesky)/cholesky | solution.py:77
  352.1 13.8 %multiply_add_fusion = f32[80,32,8,128]{3,1,2,0:T(8,128)S(1)} fusion(bf16[80,32,8,128]{3,1,2,0:T(8,128)(2,1)} %copy-done.2, bf16[80,32,2,128]{3,1,2,0:T(8,128)(2,1)S(1)} %collective-permute-done.5, bf16[80,32,2,128]{3,1,2,0:T(8,128)(2,1)S(1)} %collective-permute-done.4, f32[]{:T(128)} %bitcast.15, f32[]{:T(128)} %bitcast.14, f32[]{:T(128)} %bitcast.13, ...), kind=kLoop, calls=%fused_computation.45 | loop fusion | flops 44564480 | bytes 18350096 | tf_op jit(solution)/shard_map/add | solution.py:27
  365.9 9.6 %fusion.46 = (f32[80,32,8,2]{3,1,2,0:T(8,128)}, f32[80,32,8,2]{3,1,2,0:T(8,128)}) fusion(f32[80,32,8,128]{3,1,2,0:T(8,128)S(1)} %multiply_add_fusion), kind=kLoop, calls=%fused_computation.87 | loop fusion | bytes 655360 | tf_op jit(solution)/shard_map/slice | solution.py:15
  376.2 7.5 %copy.63 = f32[80,32,8,2]{0,2,3,1:T(8,128)S(1)} copy(f32[80,32,8,2]{3,1,2,0:T(8,128)} %get-tuple-element.11) | data formatting | bytes 327680 | tf_op jit(solution)/shard_map/slice | solution.py:14
  383.6 5.5 %collective-permute-start.7 = (f32[80,32,8,2]{0,2,3,1:T(8,128)S(1)}, f32[80,32,8,2]{0,2,3,1:T(8,128)S(1)}, u32[]{:S(2)}, u32[]{:S(2)}) collective-permute-start(f32[80,32,8,2]{0,2,3,1:T(8,128)S(1)} %copy.63), channel_id=1, source_target_pairs={{0,8},{8,16},{16,24},{1,9},{9,17},{17,25},{2,10},{10,18},{18,26},{... | collective-permute-start | bytes 491528 | tf_op jit(solution)/shard_map/ppermute | solution.py:16
  389.1 7.5 %copy.61 = f32[80,32,8,2]{0,2,3,1:T(8,128)S(1)} copy(f32[80,32,8,2]{3,1,2,0:T(8,128)} %get-tuple-element.10) | data formatting | bytes 327680 | tf_op jit(solution)/shard_map/slice | solution.py:15
  399.7 9.1 %copy.64 = f32[80,32,8,2]{3,1,2,0:T(8,128)} copy(f32[80,32,8,2]{0,2,3,1:T(8,128)S(1)} %collective-permute-done.7) | data formatting | bytes 327680 | tf_op jit(solution)/shard_map/ppermute | solution.py:16
  408.9 9.2 %copy.62 = f32[80,32,8,2]{3,1,2,0:T(8,128)} copy(f32[80,32,8,2]{0,2,3,1:T(8,128)S(1)} %collective-permute-done.6) | data formatting | bytes 327680 | tf_op jit(solution)/shard_map/ppermute | solution.py:17
  418.1 50.0 %bitcast_add_fusion = f32[80,32,8,128]{3,1,2,0:T(8,128)} fusion(bf16[80,32,8,128]{3,2,1,0:T(8,128)(2,1)} %param.10, f32[80,32,8,2]{3,1,2,0:T(8,128)} %copy.64, f32[80,32,8,128]{3,1,2,0:T(8,128)} %copy-done.1, f32[80,32,8,2]{3,1,2,0:T(8,128)} %copy.62, f32[]{:T(128)} %bitcast.11, f32[]{:T(128)} %bitcast.10, f32[]{:T(128)} %bitcast.9, f32[]{:T(128)} %bitcast.8, ...), kind=kOutput, calls=%fused_computation.44 | convolution fusion | flops 207093760 | bytes 26544144 | tf_op jit(solution)/shard_map/kl,mkab->mlab/dot_general | solution.py:66
  468.1 18.3 %copy.71 = f32[80,32,8,128]{3,2,1,0:T(8,128)} copy(f32[80,32,8,128]{3,1,2,0:T(8,128)} %bitcast_add_fusion) | data formatting | bytes 20971520
  (45 shorter events, 11.7 us)
Async XLA Ops:
  0.6 0.7 copy-start
  18.8 22.0 %copy-start.8 = (f32[4]{0:T(128)S(1)}, f32[4]{0:T(128)}, u32[]{:S(2)}) copy-start(f32[4]{0:T(128)} %param.13) | copy-start | bytes 52
  26.4 15.1 %collective-permute-start.1 = (bf16[80,32,8,2]{0,2,3,1:T(8,128)(2,1)S(1)}, bf16[80,32,8,2]{0,2,3,1:T(8,128)(2,1)S(1)}, u32[]{:S(2)}, u32[]{:S(2)}) collective-permute-start(bf16[80,32,8,2]{0,2,3,1:T(8,128)(2,1)S(1)} %copy.57), channel_id=1, source_target_pairs={{8,0},{16,8},{24,16},{9,1},{17,9},{25,17},{10,2},{18,10},{26,18},{... | collective-permute-start | bytes 245768 | tf_op jit(solution)/shard_map/ppermute | solution.py:17
  35.9 14.9 %collective-permute-start = (bf16[80,32,8,2]{0,2,3,1:T(8,128)(2,1)S(1)}, bf16[80,32,8,2]{0,2,3,1:T(8,128)(2,1)S(1)}, u32[]{:S(2)}, u32[]{:S(2)}) collective-permute-start(bf16[80,32,8,2]{0,2,3,1:T(8,128)(2,1)S(1)} %copy.55), channel_id=1, source_target_pairs={{0,8},{8,16},{16,24},{1,9},{9,17},{17,25},{2,10},{10,18},{18,26},{... | collective-permute-start | bytes 245768 | tf_op jit(solution)/shard_map/ppermute | solution.py:16
  90.1 5.0 %copy-start.6 = (s32[1,1,2048]{2,1,0:T(1,128)S(1)}, s32[1,1,2048]{2,1,0:T(1,128)}, u32[]{:S(2)}) copy-start(s32[1,1,2048]{2,1,0:T(1,128)} %param.17) | copy-start | bytes 24580
  90.1 5.7 %copy-start.9 = (f32[4]{0:T(128)S(1)}, f32[4]{0:T(128)}, u32[]{:S(2)}) copy-start(f32[4]{0:T(128)} %param.14) | copy-start | bytes 52
  90.1 6.3 %copy-start.7 = (s32[1,1,2048]{2,1,0:T(1,128)S(1)}, s32[1,1,2048]{2,1,0:T(1,128)}, u32[]{:S(2)}) copy-start(s32[1,1,2048]{2,1,0:T(1,128)} %param.15) | copy-start | bytes 24580
  90.8 114.1 %collective-permute-start.3 = (f32[80,32,2,128]{3,1,2,0:T(8,128)S(1)}, f32[80,32,2,128]{3,1,2,0:T(8,128)S(1)}, u32[]{:S(2)}, u32[]{:S(2)}) collective-permute-start(f32[80,32,2,128]{3,1,2,0:T(8,128)S(1)} %get-tuple-element.13), channel_id=1, source_target_pairs={{1,0},{2,1},{3,2},{4,3},{5,4},{6,5},{7,6},{0,7},{9,8},{10,9},{11,1... | collective-permute-start | bytes 7864328 | tf_op jit(solution)/shard_map/ppermute | solution.py:17
  95.1 110.6 %collective-permute-start.2 = (f32[80,32,2,128]{3,1,2,0:T(8,128)S(1)}, f32[80,32,2,128]{3,1,2,0:T(8,128)S(1)}, u32[]{:S(2)}, u32[]{:S(2)}) collective-permute-start(f32[80,32,2,128]{3,1,2,0:T(8,128)S(1)} %get-tuple-element.12), channel_id=1, source_target_pairs={{0,1},{1,2},{2,3},{3,4},{4,5},{5,6},{6,7},{7,0},{8,9},{9,10},{10,1... | collective-permute-start | bytes 7864328 | tf_op jit(solution)/shard_map/ppermute | solution.py:16
  205.7 1.5 copy-start.3
  207.2 23.5 %copy-start.4 = (f32[1,1,2048]{2,1,0:T(1,128)S(1)}, f32[1,1,2048]{2,1,0:T(1,128)}, u32[]{:S(2)}) copy-start(f32[1,1,2048]{2,1,0:T(1,128)} %param.19) | copy-start | bytes 24580
  207.2 23.5 %copy-start.5 = (f32[1,1,2048]{2,1,0:T(1,128)S(1)}, f32[1,1,2048]{2,1,0:T(1,128)}, u32[]{:S(2)}) copy-start(f32[1,1,2048]{2,1,0:T(1,128)} %param.18) | copy-start | bytes 24580
  246.5 2.3 copy-start.2
  250.8 101.2 %collective-permute-start.5 = (bf16[80,32,2,128]{3,1,2,0:T(8,128)(2,1)}, bf16[80,32,2,128]{3,1,2,0:T(8,128)(2,1)S(1)}, u32[]{:S(2)}, u32[]{:S(2)}) collective-permute-start(bf16[80,32,2,128]{3,1,2,0:T(8,128)(2,1)} %get-tuple-element.15), channel_id=1, source_target_pairs={{0,1},{1,2},{2,3},{3,4},{4,5},{5,6},{6,7},{7,0},{8,9},{9,10},{10,1... | collective-permute-start | bytes 3932168 | tf_op jit(solution)/shard_map/ppermute | solution.py:16
  253.0 99.1 %collective-permute-start.4 = (bf16[80,32,2,128]{3,1,2,0:T(8,128)(2,1)}, bf16[80,32,2,128]{3,1,2,0:T(8,128)(2,1)S(1)}, u32[]{:S(2)}, u32[]{:S(2)}) collective-permute-start(bf16[80,32,2,128]{3,1,2,0:T(8,128)(2,1)} %get-tuple-element.14), channel_id=1, source_target_pairs={{1,0},{2,1},{3,2},{4,3},{5,4},{6,5},{7,6},{0,7},{9,8},{10,9},{11,1... | collective-permute-start | bytes 3932168 | tf_op jit(solution)/shard_map/ppermute | solution.py:17
  365.9 10.2 %copy-start.1 = (f32[80,32,8,128]{3,1,2,0:T(8,128)}, f32[80,32,8,128]{3,1,2,0:T(8,128)S(1)}, u32[]{:S(2)}) copy-start(f32[80,32,8,128]{3,1,2,0:T(8,128)S(1)} %multiply_add_fusion) | copy-start | bytes 31457284
  383.6 16.1 %collective-permute-start.7 = (f32[80,32,8,2]{0,2,3,1:T(8,128)S(1)}, f32[80,32,8,2]{0,2,3,1:T(8,128)S(1)}, u32[]{:S(2)}, u32[]{:S(2)}) collective-permute-start(f32[80,32,8,2]{0,2,3,1:T(8,128)S(1)} %copy.63), channel_id=1, source_target_pairs={{0,8},{8,16},{16,24},{1,9},{9,17},{17,25},{2,10},{10,18},{18,26},{... | collective-permute-start | bytes 491528 | tf_op jit(solution)/shard_map/ppermute | solution.py:16
  396.6 12.3 %collective-permute-start.6 = (f32[80,32,8,2]{0,2,3,1:T(8,128)S(1)}, f32[80,32,8,2]{0,2,3,1:T(8,128)S(1)}, u32[]{:S(2)}, u32[]{:S(2)}) collective-permute-start(f32[80,32,8,2]{0,2,3,1:T(8,128)S(1)} %copy.61), channel_id=1, source_target_pairs={{8,0},{16,8},{24,16},{9,1},{17,9},{25,17},{10,2},{18,10},{26,18},{... | collective-permute-start | bytes 491528 | tf_op jit(solution)/shard_map/ppermute | solution.py:17
where the time goes:
time: 493 us; the launch traced here: 487 us
  local copies, waits for them, and re-layouts  148 us (30%)
  waiting for transfers between devices  109 us (22%)
  other arithmetic  80.5 us (16%)
  blocking collectives  65.3 us (13%)
  matrix products  58.7 us (12%)
  starting transfers between devices  23.2 us (5%)
    ppermute x4, waiting for transfers between devices, with_halo(): after = lax.ppermute(leading, axis, down)  108 us
    psum x1, blocking collectives, shards(): summed_gram = lax.psum(local_gram, ('lat', 'lon'))  65.3 us
    dot_general x1, matrix products, shards(): jnp.einsum('kl,mkab->mlab', level_mix, spread.astype(jnp.bfloat16), prefe...  50 us
    add x2, other arithmetic, taps_along(): summed = summed + weights[position] * piece.astype(jnp.float32)  43.9 us
    unnamed x22, local copies, waits for them, and re-layouts  34.1 us
    slice x4, local copies, waits for them, and re-layouts, with_halo(): last = lax.slice_in_dim(shard, length - width, length, axis=dim)  26.8 us
    slice x4, local copies, waits for them, and re-layouts, with_halo(): leading = lax.slice_in_dim(shard, 0, width, axis=dim)  26.7 us
    ppermute x2, local copies, waits for them, and re-layouts, with_halo(): after = lax.ppermute(leading, axis, down)  18.5 us
  transfers between devices with their start and end apart: 8, of which 2 were waited for; matrix products, arithmetic and copies ran while one was open for 14% of the time, Pallas kernels for 0%

commit v1 on v0

v1 whole, which is shorter than its diff:
```python
import jax
import jax.numpy as jnp
from jax import lax
from jax.experimental import pallas as pl
from jax.experimental.pallas import tpu as pltpu
from jax.sharding import PartitionSpec as P

OFFSETS = (-2, -1, 1, 2)
F32, BF = jnp.float32, jnp.bfloat16
VMEM_LIMIT = 56 * 1024 * 1024


def split2(x):
    hi = lax.reduce_precision(x, 8, 7)
    return hi.astype(BF), (x - hi).astype(BF)


def tap_of(diff, taps):
    out = (diff == 0).astype(F32)
    for t in range(4):
        out = out + jnp.where(diff == OFFSETS[t], taps[t], 0.0)
    return out


def nn(a, b):
    return jnp.dot(a, b, preferred_element_type=F32)


def nt(a, b):
    return lax.dot_general(a, b, (((1,), (1,)), ((), ())), preferred_element_type=F32)


def tn(a, b):
    return lax.dot_general(a, b, (((0,), (0,)), ((), ())), preferred_element_type=F32)


def part3(x):
    a = x.astype(BF)
    r = x - a.astype(F32)
    b = r.astype(BF)
    c = (r - b.astype(F32)).astype(BF)
    return a, b, c


def edge_kernel(c_ref, e_ref, sel_ref, perm_ref, ce_ref, ee_ref, lo_ref, hi_ref):
    half = lo_ref.shape[1]
    for m in range(c_ref.shape[0]):
        e = e_ref[m]
        ce_ref[m] = nt(sel_ref[...], c_ref[m]).astype(BF)
        ee_ref[m] = nt(sel_ref[...], e).astype(BF)
        picked = nn(perm_ref[...], e).astype(BF)
        lo_ref[m] = picked[:half]
        hi_ref[m] = picked[half:]


def forward_kernel(
    c_ref, e_ref, ch_ref, kl_ref, klt_ref, lf_ref, bf_ref, lh_ref, ll_ref, inc_ref, left_ref, right_ref
):
    rows = c_ref.shape[1]
    lanes = c_ref.shape[2]
    half = left_ref.shape[1]

    @pl.when(pl.program_id(0) == 0)
    def _():
        inc_ref[...] = jnp.zeros_like(inc_ref)

    halo = nn(ch_ref[...], klt_ref[...])
    total = jnp.zeros((rows, lanes), F32)
    for pair in range(c_ref.shape[0] // 2):
        m0 = 2 * pair
        wide = jnp.concatenate([c_ref[m0], c_ref[m0 + 1]], axis=1)
        mixed = nn(kl_ref[...], wide).astype(BF)
        row = []
        for i in range(2):
            y = nn(mixed[:, i * lanes : (i + 1) * lanes], lf_ref[...])
            edge = tn(halo[8 * (m0 + i) : 8 * (m0 + i) + 8].astype(BF), bf_ref[...])
            row.append((y[:, :lanes] + y[:, lanes:] + edge).astype(BF))
        row = jnp.concatenate(row, axis=1)
        loc = nn(lh_ref[...], row) + nn(ll_ref[...], row)
        for i in range(2):
            cut = loc[:, i * lanes : (i + 1) * lanes]
            total = total + e_ref[m0 + i].astype(F32) * cut[:rows]
            left_ref[m0 + i] = cut[rows : rows + half].astype(BF)
            right_ref[m0 + i] = cut[rows + half :].astype(BF)
    inc_ref[...] += total


def obs_kernel(inc_ref, place_ref, q_ref, innov_ref, pulled_ref, edge_ref):
    rows, lanes = inc_ref.shape
    slots = place_ref.shape[1]
    place = place_ref[...]
    r = place // lanes
    c = place - r * lanes
    rt = (lax.broadcasted_iota(jnp.int32, (rows, slots), 0) == r).astype(F32).astype(BF)
    lane_ids = lax.broadcasted_iota(jnp.int32, (lanes, slots), 0)
    hit = lane_ids == c
    inc_t = inc_ref[...].T
    g = jnp.zeros((lanes, slots), F32)
    for part in part3(inc_t):
        g = g + nn(part, rt)
    at_slot = jnp.sum(jnp.where(hit, g, 0.0), axis=0, keepdims=True)
    misfit = q_ref[...] * (at_slot - innov_ref[...])
    e_ids = lax.broadcasted_iota(jnp.int32, (8, slots), 0)
    e_lane = jnp.where(e_ids < 2, e_ids, lanes - 4 + e_ids)
    e_hit = (e_lane == c) & (e_ids < 4)
    pulled = jnp.zeros((rows, lanes), F32)
    edge = jnp.zeros((8, rows), F32)
    for part in part3(misfit):
        part = part.astype(F32)
        pulled = pulled + nt(rt, jnp.where(hit, part, 0.0).astype(BF))
        edge = edge + nt(jnp.where(e_hit, part, 0.0).astype(BF), rt)
    pulled_ref[...] = pulled
    edge_ref[...] = edge


def adjoint_kernel(
    c_ref, e_ref, el_ref, er_ref, elat_ref, p_ref, pl_ref, pr_ref, plat_ref,
    th_ref, tl_ref, xh_ref, xl_ref, la_ref, ba_ref, klt_ref, out_ref,
):
    lanes = c_ref.shape[2]
    count = c_ref.shape[0]
    plat = jnp.concatenate([plat_ref[...]] * count, axis=0)
    plane = (elat_ref[...].astype(F32) * plat).astype(BF)
    halo = nn(plane, xh_ref[...]) + nn(plane, xl_ref[...])
    for pair in range(count // 2):
        m0 = 2 * pair
        ext = []
        for i in range(2):
            ext.append(
                jnp.concatenate(
                    [
                        (e_ref[m0 + i].astype(F32) * p_ref[...]).astype(BF),
                        (el_ref[m0 + i].astype(F32) * pl_ref[...]).astype(BF),
                        (er_ref[m0 + i].astype(F32) * pr_ref[...]).astype(BF),
                    ],
                    axis=0,
                )
            )
        ext = jnp.concatenate(ext, axis=1)
        col = (nn(th_ref[...], ext) + nn(tl_ref[...], ext)).astype(BF)
        spread = []
        for i in range(2):
            y = nn(col[:, i * lanes : (i + 1) * lanes], la_ref[...])
            edge = tn(halo[8 * (m0 + i) : 8 * (m0 + i) + 8].astype(BF), ba_ref[...])
            spread.append((y[:, :lanes] + y[:, lanes:] + edge).astype(BF))
        back = nn(klt_ref[...], jnp.concatenate(spread, axis=1))
        for i in range(2):
            out_ref[m0 + i] = c_ref[m0 + i].astype(F32) + back[:, i * lanes : (i + 1) * lanes]


def full(shape):
    return pl.BlockSpec(shape, lambda g: (0,) * len(shape))


def shift(x, axis, step, wrap):
    n = lax.axis_size(axis)
    if step > 0:
        pairs = [(i, (i + 1) % n) for i in range(n if wrap else n - 1)]
    else:
        pairs = [((i + 1) % n, i) for i in range(n if wrap else n - 1)]
    return lax.ppermute(x, axis, pairs)


def shards(
    control, ensemble, level_mix, lat_taps, lon_taps, obs_location, obs_count, obs_keep, innovation, obs_weight
):
    members, levels, cols, lanes = control.shape
    rows = levels * cols
    half = 2 * levels
    ext = rows + 2 * half
    block = 8 if members % 8 == 0 else 2
    steps = members // block
    c3 = control.reshape(members, rows, lanes)
    e3 = ensemble.reshape(members, rows, lanes)
    params = pltpu.CompilerParams(vmem_limit_bytes=VMEM_LIMIT)

    own = jnp.arange(rows)
    own_level, own_col = own // cols, own % cols
    h = jnp.arange(half)
    ext_level = jnp.concatenate([own_level, h // 2, h // 2])
    ext_col = jnp.concatenate([own_col, h % 2 - 2, cols + h % 2])
    same = ext_level[:, None] == own_level[None, :]
    lon_mat = jnp.where(same, tap_of(own_col[None, :] - ext_col[:, None], lon_taps), 0.0)
    lon_hi, lon_lo = split2(lon_mat)
    lane_id = jnp.arange(lanes)
    edge_pos = jnp.array([-2, -1, lanes, lanes + 1])
    lf_hi, lf_lo = split2(tap_of(lane_id[:, None] - lane_id[None, :], lat_taps))
    lf = jnp.concatenate([lf_hi, lf_lo], axis=1)
    la = jnp.concatenate([lf_hi.T, lf_lo.T], axis=1)
    bf = jnp.concatenate(split2(tap_of(edge_pos[:, None] - lane_id[None, :], lat_taps)), axis=0)
    ba = jnp.concatenate(split2(tap_of(lane_id[None, :] - edge_pos[:, None], lat_taps)), axis=0)
    kl = jnp.where(
        own_col[:, None] == own_col[None, :], jnp.repeat(jnp.repeat(level_mix, cols, 0), cols, 1), 0
    ).astype(BF)
    klt = kl.T
    sel_id = jnp.arange(8)
    sel_lane = jnp.where(sel_id < 2, sel_id, jnp.where(sel_id < 4, lanes - 4 + sel_id, -1))
    sel = (sel_lane[:, None] == lane_id[None, :]).astype(BF)
    pick_level = jnp.concatenate([h // 2, h // 2])
    pick_col = jnp.concatenate([h % 2, cols - 2 + h % 2])
    perm = (pick_level * cols + pick_col)[:, None] == own[None, :]
    perm = perm.astype(BF)

    member_block = lambda a, b: pl.BlockSpec((block, a, b), lambda g: (g, 0, 0))
    ce, ee, low, high = pl.pallas_call(
        edge_kernel,
        grid=(steps,),
        in_specs=[member_block(rows, lanes)] * 2 + [full((8, lanes)), full((2 * half, rows))],
        out_specs=[member_block(8, rows)] * 2 + [member_block(half, lanes)] * 2,
        out_shape=[jax.ShapeDtypeStruct((members, 8, rows), BF)] * 2
        + [jax.ShapeDtypeStruct((members, half, lanes), BF)] * 2,
        compiler_params=params,
        cost_estimate=pl.CostEstimate(flops=10**9, bytes_accessed=13 * 10**6, transcendentals=0),
    )(c3, e3, sel, perm)

    both = jnp.concatenate([ce, ee], axis=0)
    before = shift(both[:, 2:4], "lat", 1, False)
    after = shift(both[:, 0:2], "lat", -1, False)
    lat_halo = jnp.concatenate([before, after], axis=1)
    lat_halo = jnp.concatenate([lat_halo, lat_halo], axis=1)
    ch, eh = lat_halo[:members], lat_halo[members:]
    e_left = shift(high, "lon", 1, True)
    e_right = shift(low, "lon", -1, True)
    corner = nt(eh.reshape(members * 8, rows), perm).astype(BF).reshape(members, 8, 2 * half)
    x_left = shift(corner[:, :4, half:], "lon", 1, True)
    x_right = shift(corner[:, :4, :half], "lon", -1, True)
    x_both = jnp.concatenate([x_left, x_right], axis=2)
    elat = jnp.concatenate([eh, jnp.concatenate([x_both, x_both], axis=1)], axis=2).reshape(members * 8, ext)

    inc, left, right = pl.pallas_call(
        forward_kernel,
        grid=(steps,),
        in_specs=[member_block(rows, lanes)] * 2
        + [pl.BlockSpec((block * 8, rows), lambda g: (g, 0)), full((rows, rows)), full((rows, rows))]
        + [full((lanes, 2 * lanes)), full((8, lanes)), full((ext, rows)), full((ext, rows))],
        out_specs=[full((rows, lanes))] + [member_block(half, lanes)] * 2,
        out_shape=[jax.ShapeDtypeStruct((rows, lanes), F32)]
        + [jax.ShapeDtypeStruct((members, half, lanes), BF)] * 2,
        compiler_params=params,
        cost_estimate=pl.CostEstimate(flops=10**10, bytes_accessed=20 * 10**6, transcendentals=0),
    )(c3, e3, ch.reshape(members * 8, rows), kl, klt, lf, bf, lon_hi, lon_lo)

    places = obs_location[0, 0]
    slots = places.shape[0]
    slot_ids = jnp.arange(slots, dtype=jnp.int32)
    live = (slot_ids < obs_count[0, 0]).astype(F32) * obs_keep[0, 0].astype(F32)
    q = live * obs_weight[0, 0]
    columns = ensemble.reshape(members, -1)[:, places]
    scaled = columns.astype(F32) * jnp.sqrt(q)[None, :]
    local_gram = jnp.dot(scaled, scaled.T, precision=lax.Precision.HIGHEST)
    total_obs = slots * lax.axis_size("lat") * lax.axis_size("lon")
    gram = lax.psum(local_gram, ("lat", "lon"))
    upper = jnp.linalg.cholesky(jnp.eye(members, dtype=F32) + members / total_obs * gram).T

    to_left = jnp.sum(e_left.astype(F32) * left.astype(F32), axis=0)
    to_right = jnp.sum(e_right.astype(F32) * right.astype(F32), axis=0)
    from_right = shift(to_left, "lon", -1, True)
    from_left = shift(to_right, "lon", 1, True)
    cube = inc.reshape(levels, cols, lanes)
    zeros = jnp.zeros((levels, cols - 2, lanes), F32)
    cube = (
        cube
        + jnp.concatenate([from_left.reshape(levels, 2, lanes), zeros], axis=1)
        + jnp.concatenate([zeros, from_right.reshape(levels, 2, lanes)], axis=1)
    )

    pulled, p_edge = pl.pallas_call(
        obs_kernel,
        out_shape=[jax.ShapeDtypeStruct((rows, lanes), F32), jax.ShapeDtypeStruct((8, rows), F32)],
        compiler_params=params,
    )(cube.reshape(rows, lanes), places[None], q[None], innovation[0])

    p_before = shift(p_edge[2:4], "lat", 1, False)
    p_after = shift(p_edge[0:2], "lat", -1, False)
    plat = jnp.concatenate([p_before, p_after], axis=0)
    plat3 = plat.reshape(4, levels, cols)
    p3 = pulled.reshape(levels, cols, lanes)
    p_left = shift(p3[:, cols - 2 :].reshape(half, lanes), "lon", 1, True)
    p_right = shift(p3[:, :2].reshape(half, lanes), "lon", -1, True)
    px_left = shift(plat3[:, :, cols - 2 :].reshape(4, half), "lon", 1, True)
    px_right = shift(plat3[:, :, :2].reshape(4, half), "lon", -1, True)
    plat = jnp.concatenate([plat, px_left, px_right], axis=1)
    plat = jnp.concatenate([plat, plat], axis=0)

    gradient = pl.pallas_call(
        adjoint_kernel,
        grid=(steps,),
        in_specs=[member_block(rows, lanes)] * 2
        + [member_block(half, lanes)] * 2
        + [pl.BlockSpec((block * 8, ext), lambda g: (g, 0))]
        + [full((rows, lanes)), full((half, lanes)), full((half, lanes)), full((8, ext))]
        + [full((rows, ext))] * 2
        + [full((ext, rows))] * 2
        + [full((lanes, 2 * lanes)), full((8, lanes)), full((rows, rows))],
        out_specs=member_block(rows, lanes),
        out_shape=jax.ShapeDtypeStruct((members, rows, lanes), F32),
        compiler_params=params,
        cost_estimate=pl.CostEstimate(flops=10**10, bytes_accessed=24 * 10**6, transcendentals=0),
    )(c3, e3, e_left, e_right, elat, pulled, p_left, p_right, plat,
      lon_hi.T, lon_lo.T, lon_hi, lon_lo, la, ba, klt)
    return gradient.reshape(members, levels, cols, lanes), upper


def solution(mesh):
    in_specs = (
        P(None, None, "lon", "lat"),
        P(None, None, "lon", "lat"),
        P(),
        P(),
        P(),
        P("lon", "lat", None),
        P("lon", "lat"),
        P("lon", "lat", None),
        P("lon", "lat", None),
        P("lon", "lat", None),
    )
    out_specs = (P(None, None, "lon", "lat"), P())
    return jax.shard_map(shards, mesh=mesh, in_specs=in_specs, out_specs=out_specs, check_vma=False)
```

time: 493 us -> 212 us (0.43)
  local copies, waits for them, and re-layouts: 148 us -> 29.7 us
  waiting for transfers between devices: 109 us -> 1.98 us
  Pallas kernels: 0 us -> 61.6 us
  matrix products: 58.7 us -> 3.31 us
  other arithmetic: 80.5 us -> 39.9 us
  blocking collectives: 65.3 us -> 38.4 us
  starting transfers between devices: 23.2 us -> 32.5 us
    ppermute x8 -> x14, waiting for transfers between devices: 109 us -> 1.98 us  [shift(): return lax.ppermute(x, axis, pairs)]
    pallas_call x0 -> x4, Pallas kernels: none -> 61.6 us  [the longest x1 25.3 us: shards(): pl.pallas_call(adjoint_kernel, grid=(steps,), in_specs=[member_block(rows...]
    dot_general x2 -> x1, matrix products: 56.3 us -> 0.31 us  [nt(): lax.dot_general(a, b, (((1,), (1,)), ((), ())), preferred_element_type=F32)]
    slice x10 -> x9, local copies, waits for them, and re-layouts: 54.8 us -> 3.81 us  [the longest x2 1.33 us: tap_of(): out = out + jnp.where(diff == OFFSETS[t], taps[t], 0.0)]
    add x3 -> x4, other arithmetic: 43.9 us -> 0.1 us  [the longest x1 0.08 us: shards(): perm = (pick_level * cols + pick_col)[:, None] == own[None, :]]
    ppermute x4 -> x0, local copies, waits for them, and re-layouts: 36.9 us -> none  [the longest x2 18.5 us: with_halo(): after = lax.ppermute(leading, axis, down)]
    psum x1, blocking collectives: 65.3 us -> 38.4 us  [shards(): gram = lax.psum(local_gram, ('lat', 'lon'))]
    unnamed x22 -> x36, local copies, waits for them, and re-layouts: 34.1 us -> 12.9 us
  transfers between devices with their start and end apart: 8 -> 14, of which waited for: 2 -> 2; matrix products, arithmetic and copies ran while one was open for 14% -> 33% of each run, Pallas kernels for 0% -> 12%
where the time goes in v1:
time: 212 us; the launch traced here: 209 us
  Pallas kernels  61.6 us (29%)
  other arithmetic  39.9 us (19%)
  blocking collectives  38.4 us (18%)
  starting transfers between devices  32.5 us (15%)
  local copies, waits for them, and re-layouts  29.7 us (14%)
  matrix products  3.31 us (2%)
    psum x1, blocking collectives, shards(): gram = lax.psum(local_gram, ('lat', 'lon'))  38.4 us
    ppermute x14, starting transfers between devices, shift(): return lax.ppermute(x, axis, pairs)  32.5 us
    pallas_call x1, Pallas kernels, shards(): pl.pallas_call(adjoint_kernel, grid=(steps,), in_specs=[member_block(rows...  25.3 us
    pallas_call x1, Pallas kernels, shards(): pl.pallas_call(forward_kernel, grid=(steps,), in_specs=[member_block(rows...  21.5 us
    convert_element_type x5, other arithmetic, split2(): return (hi.astype(BF), (x - hi).astype(BF))  15.7 us
    unnamed x36, local copies, waits for them, and re-layouts  12.9 us
    pallas_call x1, Pallas kernels, shards(): pl.pallas_call(edge_kernel, grid=(steps,), in_specs=[member_block(rows, l...  10.6 us
    gather x1, local copies, waits for them, and re-layouts, shards(): columns = ensemble.reshape(members, -1)[:, places]  10.1 us
  transfers between devices with their start and end apart: 14, of which 2 were waited for; matrix products, arithmetic and copies ran while one was open for 33% of the time, Pallas kernels for 12%

profile of v1, /device:TPU:1, one launch (start us, length us, event | category | flops | bytes accessed | tf_op | source)
XLA Modules:
  0.0 209.0 jit_solution(4153778388613038165)
XLA Ops:
  2.1 10.6 %shard_map.122 = (bf16[80,8,256]{2,1,0:T(8,128)(2,1)}, bf16[80,8,256]{2,1,0:T(8,128)(2,1)}, bf16[80,64,128]{2,1,0:T(8,128)(2,1)}, bf16[80,64,128]{2,1,0:T(8,128)(2,1)}) custom-call(bf16[80,256,128]{2,1,0:T(8,128)(2,1)} %bitcast.68, bf16[80,256,128]{2,1,0:T(8,128)(2,1)} %bitcast.64, bf16[8,128]{1,0:T(8,128)(2,1)} %fusion.26.sel_ref, ...), custom_call_target="tpu_custom_call" | custom-call | flops 1000000000 | bytes 13000000 | tf_op jit(solution)/shard_map/pallas_call | solution.py:205
  12.8 2.1 collective-permute-start
  14.9 3.1 %collective-permute-start.1 = (bf16[80,64,128]{2,1,0:T(8,128)(2,1)}, bf16[80,64,128]{2,1,0:T(8,128)(2,1)S(1)}, u32[]{:S(2)}, u32[]{:S(2)}) collective-permute-start(bf16[80,64,128]{2,1,0:T(8,128)(2,1)} %get-tuple-element.12), channel_id=1, source_target_pairs={{1,0},{2,1},{3,2},{4,3},{5,4},{6,5},{7,6},{0,7},{9,8},{10,9},{11,1... | collective-permute-start | bytes 3932168 | tf_op jit(solution)/shard_map/ppermute | solution.py:161
  18.0 1.0 constant_dynamic-update-slice_fusion.1
  19.0 1.0 constant_dynamic-update-slice_fusion
  20.8 2.9 %collective-permute-start.3 = (bf16[160,2,256]{2,1,0:T(2,128)(2,1)}, bf16[160,2,256]{2,1,0:T(2,128)(2,1)}, u32[]{:S(2)}, u32[]{:S(2)}) collective-permute-start(bf16[160,2,256]{2,1,0:T(2,128)(2,1)} %get-tuple-element.23), channel_id=1, source_target_pairs={{8,0},{16,8},{24,16},{9,1},{17,9},{25,17},{10,2},{18,10},{26,18},{... | collective-permute-start | bytes 491528 | tf_op jit(solution)/shard_map/ppermute | solution.py:161
  23.7 3.2 %collective-permute-start.2 = (bf16[160,2,256]{2,1,0:T(2,128)(2,1)S(1)}, bf16[160,2,256]{2,1,0:T(2,128)(2,1)}, u32[]{:S(2)}, u32[]{:S(2)}) collective-permute-start(bf16[160,2,256]{2,1,0:T(2,128)(2,1)S(1)} %get-tuple-element.22), channel_id=1, source_target_pairs={{0,8},{8,16},{16,24},{1,9},{9,17},{17,25},{2,10},{10,18},{18,26},{... | collective-permute-start | bytes 491528 | tf_op jit(solution)/shard_map/ppermute | solution.py:161
  27.7 3.7 %fusion.5 = (bf16[384,256]{1,0:T(8,128)(2,1)}, bf16[384,256]{1,0:T(8,128)(2,1)}) fusion(f32[]{:T(128)} %bitcast.16, f32[]{:T(128)} %bitcast.15, f32[]{:T(128)} %bitcast.14, f32[]{:T(128)} %bitcast.13, s32[384]{0:T(512)S(1)} %pad_add_fusion.1, s32[256]{0:T(256)S(1)} %get-tuple-element.61, s32[256]{0:T(256)S(1)} %get-tuple-element.60, s32[384]{0:T(512)S(1)} %pad_add_fusion), kind=kLoop, calls=%fused_computation.25 | loop fusion | flops 2064384 | bytes 398352 | tf_op jit(solution)/shard_map/convert_element_type | solution.py:15
  31.4 3.6 %fusion.6 = (bf16[256,384]{1,0:T(8,128)(2,1)}, bf16[256,384]{1,0:T(8,128)(2,1)}) fusion(f32[]{:T(128)} %bitcast.16, f32[]{:T(128)} %bitcast.15, f32[]{:T(128)} %bitcast.14, f32[]{:T(128)} %bitcast.13, s32[384]{0:T(512)S(1)} %pad_add_fusion.1, s32[256]{0:T(256)S(1)} %get-tuple-element.61, s32[256]{0:T(256)S(1)} %get-tuple-element.60, s32[384]{0:T(512)S(1)} %pad_add_fusion), kind=kLoop, calls=%fused_computation.26 | loop fusion | flops 2064384 | bytes 398352 | tf_op jit(solution)/shard_map/convert_element_type | solution.py:15
  35.7 3.2 %reduce-precision_convert_fusion.3 = (bf16[128,128]{1,0:T(8,128)(2,1)S(1)}, bf16[128,128]{1,0:T(8,128)(2,1)}) fusion(f32[]{:T(128)} %bitcast.12, f32[]{:T(128)} %bitcast.11, f32[]{:T(128)} %bitcast.10, f32[]{:T(128)} %bitcast.9), kind=kLoop, calls=%fused_computation.40 | loop fusion | flops 311296 | bytes 65552 | tf_op jit(solution)/shard_map/convert_element_type | solution.py:15
  38.9 2.6 %reduce-precision_convert_fusion.2 = (bf16[128,128]{1,0:T(8,128)(2,1)S(1)}, bf16[128,128]{1,0:T(8,128)(2,1)S(1)}) fusion(f32[]{:T(128)} %bitcast.12, f32[]{:T(128)} %bitcast.11, f32[]{:T(128)} %bitcast.10, f32[]{:T(128)} %bitcast.9), kind=kLoop, calls=%fused_computation.38 | loop fusion | flops 311296 | bytes 65552 | tf_op jit(solution)/shard_map/convert_element_type | solution.py:15
  41.5 10.6 %copy.26 = bf16[80,32,8,128]{0,3,2,1:T(8,128)(2,1)} copy(bf16[80,32,8,128]{3,2,1,0:T(8,128)(2,1)} %param.12) | data formatting | bytes 10485760 | tf_op args[1]
  54.9 10.1 %gather_fusion = bf16[2048,80]{1,0:T(8,128)(2,1)S(1)} fusion(bf16[80,32768]{0,1:T(8,128)(2,1)} %bitcast.67, s32[2048]{0:T(1024)S(1)} %broadcast_clamp_fusion), kind=kCustom, calls=%fused_computation | custom fusion | bytes 663552 | tf_op jit(solution)/shard_map/gather | solution.py:248
  65.7 3.0 %fusion.1 = f32[80,80]{0,1:T(8,128)} fusion(bf16[2048,80]{1,0:T(8,128)(2,1)S(1)} %gather_fusion, f32[2048]{0:T(1024)S(1)} %multiply_sqrt_fusion), kind=kOutput, calls=%fused_computation.15 | convolution fusion | flops 157614080 | bytes 361472 | tf_op jit(solution)/shard_map/dot_general | solution.py:250
  68.7 38.4 %psum.7 = f32[80,80]{0,1:T(8,128)S(1)} all-reduce(f32[80,80]{0,1:T(8,128)} %fusion.1), channel_id=1, replica_groups=mesh['lat'=4,'lon'=8] {'lat','lon'}, use_global_device_ids=true, to_apply=%region_2.3 | all-reduce | flops 6400 | bytes 51200 | tf_op jit(solution)/shard_map/psum | solution.py:252
  107.3 7.3 %cholesky.20 = f32[80,80]{1,0:T(8,128)S(1)} custom-call(f32[80,80]{1,0:T(8,128)S(1)} %fusion.24), custom_call_target="Cholesky" | custom-call | tf_op jit(solution)/shard_map/jit(cholesky)/cholesky | solution.py:253
  115.4 1.3 select_bitcast_fusion
  116.7 1.4 pad_maximum_fusion.1.lf_ref
  118.1 2.6 %reduce-precision_convert_fusion.4 = (bf16[4,128]{1,0:T(4,128)(2,1)S(1)}, bf16[4,128]{1,0:T(4,128)(2,1)S(1)}, bf16[4,128]{1,0:T(4,128)(2,1)S(1)}, bf16[4,128]{1,0:T(4,128)(2,1)S(1)}) fusion(f32[]{:T(128)} %bitcast.12, f32[]{:T(128)} %bitcast.11, f32[]{:T(128)} %bitcast.10, f32[]{:T(128)} %bitcast.9, s32[4]{0:T(128)S(1)} %copy-done.13, s32[4]{0:T(128)S(1)} %copy-done.14), kind=kLoop, calls=%fused_computation.82 | loop fusion | flops 19456 | bytes 4144 | tf_op jit(solution)/shard_map/convert_element_type | solution.py:15
  123.3 1.9 pad_maximum_fusion
  126.3 21.5 %shard_map.123 = (f32[256,128]{1,0:T(8,128)}, bf16[80,64,128]{2,1,0:T(8,128)(2,1)}, bf16[80,64,128]{2,1,0:T(8,128)(2,1)}) custom-call(bf16[80,256,128]{2,1,0:T(8,128)(2,1)} %bitcast.69, bf16[80,256,128]{2,1,0:T(8,128)(2,1)} %bitcast.65, bf16[640,256]{1,0:T(8,128)(2,1)} %get-tuple-element.20.ch_ref, bf16[256,256]{1,0:T(8,128)(2,1)} %copy.21.kl_ref, ...), custom_call_target="tpu_custom_call" | custom-call | flops 10000000000 | bytes 20000000 | tf_op jit(solution)/shard_map/pallas_call | solution.py:230
  147.9 2.4 %multiply_reduce_fusion = f32[64,128]{1,0:T(8,128)S(1)} fusion(bf16[80,64,128]{2,1,0:T(8,128)(2,1)} %get-tuple-element.17, bf16[80,64,128]{2,1,0:T(8,128)(2,1)S(1)} %collective-permute-done.el_ref), kind=kLoop, calls=%fused_computation.1 | loop fusion | flops 2613248 | bytes 2654208 | tf_op jit(solution)/shard_map/reduce_sum | solution.py:255
  150.3 2.3 %collective-permute-start.7 = (f32[64,128]{1,0:T(8,128)S(1)}, f32[64,128]{1,0:T(8,128)S(1)}, u32[]{:S(2)}, u32[]{:S(2)}) collective-permute-start(f32[64,128]{1,0:T(8,128)S(1)} %multiply_reduce_fusion), channel_id=1, source_target_pairs={{1,0},{2,1},{3,2},{4,3},{5,4},{6,5},{7,6},{0,7},{9,8},{10,9},{11,1... | collective-permute-start | bytes 98312 | tf_op jit(solution)/shard_map/ppermute | solution.py:161
  153.8 4.2 %collective-permute-start.5 = (bf16[80,4,64]{2,1,0:T(4,128)(2,1)S(1)}, bf16[80,4,64]{2,1,0:T(4,128)(2,1)S(1)}, u32[]{:S(2)}, u32[]{:S(2)}) collective-permute-start(bf16[80,4,64]{2,1,0:T(4,128)(2,1)S(1)} %get-tuple-element.25), channel_id=1, source_target_pairs={{1,0},{2,1},{3,2},{4,3},{5,4},{6,5},{7,6},{0,7},{9,8},{10,9},{11,1... | collective-permute-start | bytes 122888 | tf_op jit(solution)/shard_map/ppermute | solution.py:161
  158.0 1.1 collective-permute-done.6
  159.8 4.2 %shard_map.124 = (f32[256,128]{1,0:T(8,128)}, f32[8,256]{1,0:T(8,128)}) custom-call(f32[256,128]{1,0:T(8,128)} %fusion.9.inc_ref, s32[1,2048]{1,0:T(1,128)} %bitcast.76, f32[1,2048]{1,0:T(1,128)} %fusion.25.q_ref, f32[1,2048]{1,0:T(1,128)} %bitcast.82), custom_call_target="tpu_custom_call" | custom-call | tf_op jit(solution)/shard_map/pallas_call | solution.py:267
  164.7 5.6 %collective-permute-start.11 = (f32[2,256]{1,0:T(2,128)S(1)}, f32[2,256]{1,0:T(2,128)S(1)}, u32[]{:S(2)}, u32[]{:S(2)}) collective-permute-start(f32[2,256]{1,0:T(2,128)S(1)} %get-tuple-element.33), channel_id=1, source_target_pairs={{8,0},{16,8},{24,16},{9,1},{17,9},{25,17},{10,2},{18,10},{26,18},{... | collective-permute-start | bytes 6152 | tf_op jit(solution)/shard_map/ppermute | solution.py:161
  170.4 2.2 %collective-permute-start.10 = (f32[2,256]{1,0:T(2,128)S(1)}, f32[2,256]{1,0:T(2,128)S(1)}, u32[]{:S(2)}, u32[]{:S(2)}) collective-permute-start(f32[2,256]{1,0:T(2,128)S(1)} %get-tuple-element.32), channel_id=1, source_target_pairs={{0,8},{8,16},{16,24},{1,9},{9,17},{17,25},{2,10},{10,18},{18,26},{... | collective-permute-start | bytes 6152 | tf_op jit(solution)/shard_map/ppermute | solution.py:161
  172.5 1.0 maximum_bitcast_fusion.elat_ref
  174.2 2.7 %collective-permute-start.13 = (f32[4,64]{1,0:T(4,128)S(1)}, f32[4,64]{1,0:T(4,128)S(1)}, u32[]{:S(2)}, u32[]{:S(2)}) collective-permute-start(f32[4,64]{1,0:T(4,128)S(1)} %copy.25), channel_id=1, source_target_pairs={{1,0},{2,1},{3,2},{4,3},{5,4},{6,5},{7,6},{0,7},{9,8},{10,9},{11,1... | collective-permute-start | bytes 3080 | tf_op jit(solution)/shard_map/ppermute | solution.py:161
  177.4 4.2 %collective-permute-start.9 = (f32[64,128]{1,0:T(8,128)S(1)}, f32[64,128]{1,0:T(8,128)S(1)}, u32[]{:S(2)}, u32[]{:S(2)}) collective-permute-start(f32[64,128]{1,0:T(8,128)S(1)} %bitcast.80), channel_id=1, source_target_pairs={{1,0},{2,1},{3,2},{4,3},{5,4},{6,5},{7,6},{0,7},{9,8},{10,9},{11,1... | collective-permute-start | bytes 98312 | tf_op jit(solution)/shard_map/ppermute | solution.py:161
  183.7 25.3 %shard_map.125 = f32[80,256,128]{2,1,0:T(8,128)} custom-call(bf16[80,256,128]{2,1,0:T(8,128)(2,1)} %bitcast.70, bf16[80,256,128]{2,1,0:T(8,128)(2,1)} %bitcast.66, bf16[80,64,128]{2,1,0:T(8,128)(2,1)} %copy-done.1, bf16[80,64,128]{2,1,0:T(8,128)(2,1)} %copy-done.2, bf16[640,384]{1,0:T(8,128)(2,1)} %maximum_bitcast_fusion.elat_ref, ...), custom_call_target="tpu_custom_call" | custom-call | flops 10000000000 | bytes 24000000 | tf_op jit(solution)/shard_map/pallas_call | solution.py:285
  (97 shorter events, 17.2 us)
Async XLA Ops:
  0.6 51.5 %copy-start = (bf16[32,32]{1,0:T(8,128)(2,1)S(1)}, bf16[32,32]{1,0:T(8,128)(2,1)}, u32[]{:S(2)}) copy-start(bf16[32,32]{1,0:T(8,128)(2,1)} %param.13) | copy-start | bytes 6148
  1.4 11.4 %copy-start.11 = (s32[128]{0:T(128)}, s32[128]{0:T(128)S(1)}, u32[]{:S(2)}) copy-start(s32[128]{0:T(128)S(1)} %fusion.40) | copy-start | bytes 1540
  12.8 14.1 %copy-start.9 = (f32[4]{0:T(128)S(1)}, f32[4]{0:T(128)}, u32[]{:S(2)}) copy-start(f32[4]{0:T(128)} %param.15) | copy-start | bytes 52
  12.8 135.1 %collective-permute-start = (bf16[80,64,128]{2,1,0:T(8,128)(2,1)}, bf16[80,64,128]{2,1,0:T(8,128)(2,1)S(1)}, u32[]{:S(2)}, u32[]{:S(2)}) collective-permute-start(bf16[80,64,128]{2,1,0:T(8,128)(2,1)} %get-tuple-element.11), channel_id=1, source_target_pairs={{0,1},{1,2},{2,3},{3,4},{4,5},{5,6},{6,7},{7,0},{8,9},{9,10},{10,1... | collective-permute-start | bytes 3932168 | tf_op jit(solution)/shard_map/ppermute | solution.py:161
  14.9 137.7 %collective-permute-start.1 = (bf16[80,64,128]{2,1,0:T(8,128)(2,1)}, bf16[80,64,128]{2,1,0:T(8,128)(2,1)S(1)}, u32[]{:S(2)}, u32[]{:S(2)}) collective-permute-start(bf16[80,64,128]{2,1,0:T(8,128)(2,1)} %get-tuple-element.12), channel_id=1, source_target_pairs={{1,0},{2,1},{3,2},{4,3},{5,4},{6,5},{7,6},{0,7},{9,8},{10,9},{11,1... | collective-permute-start | bytes 3932168 | tf_op jit(solution)/shard_map/ppermute | solution.py:161
  18.0 17.1 %copy-start.10 = (f32[4]{0:T(128)S(1)}, f32[4]{0:T(128)}, u32[]{:S(2)}) copy-start(f32[4]{0:T(128)} %param.14) | copy-start | bytes 52
  20.8 102.5 %collective-permute-start.3 = (bf16[160,2,256]{2,1,0:T(2,128)(2,1)}, bf16[160,2,256]{2,1,0:T(2,128)(2,1)}, u32[]{:S(2)}, u32[]{:S(2)}) collective-permute-start(bf16[160,2,256]{2,1,0:T(2,128)(2,1)} %get-tuple-element.23), channel_id=1, source_target_pairs={{8,0},{16,8},{24,16},{9,1},{17,9},{25,17},{10,2},{18,10},{26,18},{... | collective-permute-start | bytes 491528 | tf_op jit(solution)/shard_map/ppermute | solution.py:161
  23.7 99.6 %collective-permute-start.2 = (bf16[160,2,256]{2,1,0:T(2,128)(2,1)S(1)}, bf16[160,2,256]{2,1,0:T(2,128)(2,1)}, u32[]{:S(2)}, u32[]{:S(2)}) collective-permute-start(bf16[160,2,256]{2,1,0:T(2,128)(2,1)S(1)} %get-tuple-element.22), channel_id=1, source_target_pairs={{0,8},{8,16},{16,24},{1,9},{9,17},{17,25},{2,10},{10,18},{18,26},{... | collective-permute-start | bytes 491528 | tf_op jit(solution)/shard_map/ppermute | solution.py:161
  41.5 12.2 %copy-start.7 = (s32[1,1,2048]{2,1,0:T(1,128)S(1)}, s32[1,1,2048]{2,1,0:T(1,128)}, u32[]{:S(2)}) copy-start(s32[1,1,2048]{2,1,0:T(1,128)} %param.16) | copy-start | bytes 24580
  41.5 12.2 %copy-start.6 = (s32[1,1,2048]{2,1,0:T(1,128)S(1)}, s32[1,1,2048]{2,1,0:T(1,128)}, u32[]{:S(2)}) copy-start(s32[1,1,2048]{2,1,0:T(1,128)} %param.18) | copy-start | bytes 24580
  41.5 12.8 %copy-start.5 = (f32[1,1,2048]{2,1,0:T(1,128)S(1)}, f32[1,1,2048]{2,1,0:T(1,128)}, u32[]{:S(2)}) copy-start(f32[1,1,2048]{2,1,0:T(1,128)} %param.20) | copy-start | bytes 24580
  65.0 53.2 %copy-start.13 = (s32[4]{0:T(128)S(1)}, s32[4]{0:T(128)}, u32[]{:S(2)}) copy-start(s32[4]{0:T(128)} %constant.168) | copy-start | bytes 52
  65.0 53.1 %copy-start.14 = (s32[4]{0:T(128)S(1)}, s32[4]{0:T(128)}, u32[]{:S(2)}) copy-start(s32[4]{0:T(128)} %constant.158.clone) | copy-start | bytes 52
  121.9 4.1 %copy-start.12 = (s32[128]{0:T(128)S(1)}, s32[128]{0:T(128)}, u32[]{:S(2)}) copy-start(s32[128]{0:T(128)} %copy-done.11) | copy-start | bytes 1540
  147.9 2.4 %copy-start.1 = (bf16[80,64,128]{2,1,0:T(8,128)(2,1)}, bf16[80,64,128]{2,1,0:T(8,128)(2,1)S(1)}, u32[]{:S(2)}) copy-start(bf16[80,64,128]{2,1,0:T(8,128)(2,1)S(1)} %collective-permute-done.el_ref) | copy-start | bytes 3932164
  147.9 4.7 %copy-start.3 = (bf16[80,64,128]{2,1,0:T(8,128)(2,1)S(1)}, bf16[80,64,128]{2,1,0:T(8,128)(2,1)}, u32[]{:S(2)}) copy-start(bf16[80,64,128]{2,1,0:T(8,128)(2,1)} %get-tuple-element.16) | copy-start | bytes 3932164
  150.3 7.7 %collective-permute-start.7 = (f32[64,128]{1,0:T(8,128)S(1)}, f32[64,128]{1,0:T(8,128)S(1)}, u32[]{:S(2)}, u32[]{:S(2)}) collective-permute-start(f32[64,128]{1,0:T(8,128)S(1)} %multiply_reduce_fusion), channel_id=1, source_target_pairs={{1,0},{2,1},{3,2},{4,3},{5,4},{6,5},{7,6},{0,7},{9,8},{10,9},{11,1... | collective-permute-start | bytes 98312 | tf_op jit(solution)/shard_map/ppermute | solution.py:161
  152.6 1.1 copy-start.2
  152.6 6.5 %copy-start.4 = (f32[256,128]{1,0:T(8,128)S(1)}, f32[256,128]{1,0:T(8,128)}, u32[]{:S(2)}) copy-start(f32[256,128]{1,0:T(8,128)} %get-tuple-element.15) | copy-start | bytes 393220
  153.7 5.5 %collective-permute-start.6 = (f32[64,128]{1,0:T(8,128)S(1)}, f32[64,128]{1,0:T(8,128)S(1)}, u32[]{:S(2)}, u32[]{:S(2)}) collective-permute-start(f32[64,128]{1,0:T(8,128)S(1)} %multiply_reduce_fusion.1), channel_id=1, source_target_pairs={{0,1},{1,2},{2,3},{3,4},{4,5},{5,6},{6,7},{7,0},{8,9},{9,10},{10,1... | collective-permute-start | bytes 98312 | tf_op jit(solution)/shard_map/ppermute | solution.py:161
  153.8 18.8 %collective-permute-start.5 = (bf16[80,4,64]{2,1,0:T(4,128)(2,1)S(1)}, bf16[80,4,64]{2,1,0:T(4,128)(2,1)S(1)}, u32[]{:S(2)}, u32[]{:S(2)}) collective-permute-start(bf16[80,4,64]{2,1,0:T(4,128)(2,1)S(1)} %get-tuple-element.25), channel_id=1, source_target_pairs={{1,0},{2,1},{3,2},{4,3},{5,4},{6,5},{7,6},{0,7},{9,8},{10,9},{11,1... | collective-permute-start | bytes 122888 | tf_op jit(solution)/shard_map/ppermute | solution.py:161
  158.0 14.6 %collective-permute-start.4 = (bf16[80,4,64]{2,1,0:T(4,128)(2,1)S(1)}, bf16[80,4,64]{2,1,0:T(4,128)(2,1)S(1)}, u32[]{:S(2)}, u32[]{:S(2)}) collective-permute-start(bf16[80,4,64]{2,1,0:T(4,128)(2,1)S(1)} %get-tuple-element.24), channel_id=1, source_target_pairs={{0,1},{1,2},{2,3},{3,4},{4,5},{5,6},{6,7},{7,0},{8,9},{9,10},{10,1... | collective-permute-start | bytes 122888 | tf_op jit(solution)/shard_map/ppermute | solution.py:161
  164.0 13.3 %copy-start.8 = (f32[256,128]{1,0:T(8,128)S(1)}, f32[256,128]{1,0:T(8,128)}, u32[]{:S(2)}) copy-start(f32[256,128]{1,0:T(8,128)} %get-tuple-element.18.p_ref) | copy-start | bytes 393220
  164.7 8.9 %collective-permute-start.11 = (f32[2,256]{1,0:T(2,128)S(1)}, f32[2,256]{1,0:T(2,128)S(1)}, u32[]{:S(2)}, u32[]{:S(2)}) collective-permute-start(f32[2,256]{1,0:T(2,128)S(1)} %get-tuple-element.33), channel_id=1, source_target_pairs={{8,0},{16,8},{24,16},{9,1},{17,9},{25,17},{10,2},{18,10},{26,18},{... | collective-permute-start | bytes 6152 | tf_op jit(solution)/shard_map/ppermute | solution.py:161
  170.4 3.2 %collective-permute-start.10 = (f32[2,256]{1,0:T(2,128)S(1)}, f32[2,256]{1,0:T(2,128)S(1)}, u32[]{:S(2)}, u32[]{:S(2)}) collective-permute-start(f32[2,256]{1,0:T(2,128)S(1)} %get-tuple-element.32), channel_id=1, source_target_pairs={{0,8},{8,16},{16,24},{1,9},{9,17},{17,25},{2,10},{10,18},{18,26},{... | collective-permute-start | bytes 6152 | tf_op jit(solution)/shard_map/ppermute | solution.py:161
  174.2 7.5 %collective-permute-start.13 = (f32[4,64]{1,0:T(4,128)S(1)}, f32[4,64]{1,0:T(4,128)S(1)}, u32[]{:S(2)}, u32[]{:S(2)}) collective-permute-start(f32[4,64]{1,0:T(4,128)S(1)} %copy.25), channel_id=1, source_target_pairs={{1,0},{2,1},{3,2},{4,3},{5,4},{6,5},{7,6},{0,7},{9,8},{10,9},{11,1... | collective-permute-start | bytes 3080 | tf_op jit(solution)/shard_map/ppermute | solution.py:161
  177.3 5.1 %collective-permute-start.12 = (f32[4,64]{1,0:T(4,128)S(1)}, f32[4,64]{1,0:T(4,128)S(1)}, u32[]{:S(2)}, u32[]{:S(2)}) collective-permute-start(f32[4,64]{1,0:T(4,128)S(1)} %copy.23), channel_id=1, source_target_pairs={{0,1},{1,2},{2,3},{3,4},{4,5},{5,6},{6,7},{7,0},{8,9},{9,10},{10,1... | collective-permute-start | bytes 3080 | tf_op jit(solution)/shard_map/ppermute | solution.py:161
  177.3 5.8 %collective-permute-start.8 = (f32[64,128]{1,0:T(8,128)S(1)}, f32[64,128]{1,0:T(8,128)S(1)}, u32[]{:S(2)}, u32[]{:S(2)}) collective-permute-start(f32[64,128]{1,0:T(8,128)S(1)} %bitcast.81), channel_id=1, source_target_pairs={{0,1},{1,2},{2,3},{3,4},{4,5},{5,6},{6,7},{7,0},{8,9},{9,10},{10,1... | collective-permute-start | bytes 98312 | tf_op jit(solution)/shard_map/ppermute | solution.py:161
  177.4 5.7 %collective-permute-start.9 = (f32[64,128]{1,0:T(8,128)S(1)}, f32[64,128]{1,0:T(8,128)S(1)}, u32[]{:S(2)}, u32[]{:S(2)}) collective-permute-start(f32[64,128]{1,0:T(8,128)S(1)} %bitcast.80), channel_id=1, source_target_pairs={{1,0},{2,1},{3,2},{4,3},{5,4},{6,5},{7,6},{0,7},{9,8},{10,9},{11,1... | collective-permute-start | bytes 98312 | tf_op jit(solution)/shard_map/ppermute | solution.py:161
  183.1 0.6 copy-start.15
  183.1 0.6 copy-start.16

commit v2 on v1

v2 whole, which is shorter than its diff:
```python
import jax
import jax.numpy as jnp
import numpy as np
from jax import lax
from jax.experimental import pallas as pl
from jax.experimental.pallas import tpu as pltpu
from jax.sharding import PartitionSpec as P

OFFSETS = (-2, -1, 1, 2)
F32, BF = jnp.float32, jnp.bfloat16
VMEM_LIMIT = 56 * 1024 * 1024


def code_of(diff):
    out = np.zeros(diff.shape, np.int32)
    for t, offset in enumerate(OFFSETS):
        out[diff == offset] = t + 1
    out[diff == 0] = 5
    return out


def nn(a, b):
    return jnp.dot(a, b, preferred_element_type=F32)


def nt(a, b):
    return lax.dot_general(a, b, (((1,), (1,)), ((), ())), preferred_element_type=F32)


def tn(a, b):
    return lax.dot_general(a, b, (((0,), (0,)), ((), ())), preferred_element_type=F32)


def part3(x):
    a = x.astype(BF)
    r = x - a.astype(F32)
    b = r.astype(BF)
    c = (r - b.astype(F32)).astype(BF)
    return a, b, c


def setup_kernel(taps_ref, mix_ref, code_ref, codet_ref, ecode_ref, ecodet_ref, spread_ref, same_ref,
                 lf_ref, la_ref, bf_ref, ba_ref, xh_ref, xl_ref, kl_ref, klt_ref, xcode_ref):
    def put(code, base):
        out = jnp.where(code == 5, 1.0, 0.0)
        for t in range(4):
            out = out + jnp.where(code == t + 1, taps_ref[base + t], 0.0)
        hi = out.astype(BF)
        return hi, (out - hi.astype(F32)).astype(BF)

    lf_ref[...] = jnp.concatenate(put(code_ref[...], 0), axis=1)
    la_ref[...] = jnp.concatenate(put(codet_ref[...], 0), axis=1)
    hi, lo = put(ecode_ref[...], 0)
    top = lax.broadcasted_iota(jnp.int32, hi.shape, 0) < 4
    bf_ref[...] = jnp.where(top, hi.astype(F32), lo.astype(F32)).astype(BF)
    hi, lo = put(ecodet_ref[...], 0)
    ba_ref[...] = jnp.where(top, hi.astype(F32), lo.astype(F32)).astype(BF)
    hi, lo = put(xcode_ref[...], 4)
    xh_ref[...] = hi
    xl_ref[...] = lo
    mix = mix_ref[...]
    spread = spread_ref[...]
    same = same_ref[...].astype(F32)
    wide = nn(nn(spread, mix).astype(BF), spread.T)
    kl_ref[...] = (wide * same).astype(BF)
    wide = nn(spread, nt(mix.T, spread).astype(BF))
    klt_ref[...] = (wide * same).astype(BF)


def column_kernel(e_ref, perm_ref, lo_ref, hi_ref):
    half = lo_ref.shape[1]
    lanes = e_ref.shape[2]
    for m in range(0, e_ref.shape[0], 2):
        wide = jnp.concatenate([e_ref[m], e_ref[m + 1]], axis=1)
        picked = nn(perm_ref[...], wide).astype(BF)
        for i in range(2):
            lo_ref[m + i] = picked[:half, i * lanes : (i + 1) * lanes]
            hi_ref[m + i] = picked[half:, i * lanes : (i + 1) * lanes]


def edge_kernel(c_ref, e_ref, sel_ref, ce_ref, ee_ref):
    for m in range(c_ref.shape[0]):
        ce_ref[m] = nt(sel_ref[...], c_ref[m]).astype(BF)
        ee_ref[m] = nt(sel_ref[...], e_ref[m]).astype(BF)


def column_masks(cols, lanes, direction):
    row = lax.broadcasted_iota(jnp.int32, (1, cols, lanes), 1)
    wraps = []
    for offset in OFFSETS:
        o = direction * offset
        wraps.append((row >= cols - o) if o > 0 else (row < -o))
    return row, wraps


def forward_kernel(
    taps_ref, c_ref, e_ref, ch_ref, kl_ref, klt_ref, lf_ref, bf_ref, perm_ref, inc_ref, left_ref, right_ref
):
    rows = c_ref.shape[1]
    lanes = c_ref.shape[2]
    half = left_ref.shape[1]
    levels = half // 2
    cols = rows // levels

    @pl.when(pl.program_id(0) == 0)
    def _():
        inc_ref[...] = jnp.zeros_like(inc_ref)

    _, wraps = column_masks(cols, lanes, 1)
    inner = [jnp.where(w, 0.0, taps_ref[4 + t]) for t, w in enumerate(wraps)]
    outer = [jnp.where(w, taps_ref[4 + t], 0.0) for t, w in enumerate(wraps)]
    halo = nn(ch_ref[...], klt_ref[...])
    total = jnp.zeros((rows, lanes), F32)
    for pair in range(c_ref.shape[0] // 2):
        m0 = 2 * pair
        wide = jnp.concatenate([c_ref[m0], c_ref[m0 + 1]], axis=1)
        mixed = nn(kl_ref[...], wide).astype(BF)
        over = []
        for i in range(2):
            y = nn(mixed[:, i * lanes : (i + 1) * lanes], lf_ref[...])
            edge = tn(halo[8 * (m0 + i) : 8 * (m0 + i) + 8].astype(BF), bf_ref[...])
            row = (y[:, :lanes] + y[:, lanes:] + edge).reshape(levels, cols, lanes)
            loc = row
            out = jnp.zeros_like(row)
            for t in range(4):
                moved = pltpu.roll(row, (-OFFSETS[t]) % cols, 1)
                loc = loc + inner[t] * moved
                out = out + outer[t] * moved
            total = total + e_ref[m0 + i].astype(F32) * loc.reshape(rows, lanes)
            over.append(out.reshape(rows, lanes).astype(BF))
        picked = nn(perm_ref[...], jnp.concatenate(over, axis=1)).astype(BF)
        for i in range(2):
            right_ref[m0 + i] = picked[:half, i * lanes : (i + 1) * lanes]
            left_ref[m0 + i] = picked[half:, i * lanes : (i + 1) * lanes]
    inc_ref[...] += total


def obs_kernel(inc_ref, place_ref, q_ref, innov_ref, pulled_ref, edge_ref):
    rows, lanes = inc_ref.shape
    slots = place_ref.shape[1]
    place = place_ref[...]
    r = place // lanes
    c = place - r * lanes
    rt = (lax.broadcasted_iota(jnp.int32, (rows, slots), 0) == r).astype(F32).astype(BF)
    lane_ids = lax.broadcasted_iota(jnp.int32, (lanes, slots), 0)
    hit = lane_ids == c
    inc_t = inc_ref[...].T
    g = jnp.zeros((lanes, slots), F32)
    for part in part3(inc_t):
        g = g + nn(part, rt)
    at_slot = jnp.sum(jnp.where(hit, g, 0.0), axis=0, keepdims=True)
    misfit = q_ref[...] * (at_slot - innov_ref[...])
    e_ids = lax.broadcasted_iota(jnp.int32, (8, slots), 0)
    e_lane = jnp.where(e_ids < 2, e_ids, lanes - 4 + e_ids)
    e_hit = (e_lane == c) & (e_ids < 4)
    pulled = jnp.zeros((rows, lanes), F32)
    edge = jnp.zeros((8, rows), F32)
    for part in part3(misfit):
        part = part.astype(F32)
        pulled = pulled + nt(rt, jnp.where(hit, part, 0.0).astype(BF))
        edge = edge + nt(jnp.where(e_hit, part, 0.0).astype(BF), rt)
    pulled_ref[...] = pulled
    edge_ref[...] = edge


def adjoint_kernel(
    taps_ref, c_ref, e_ref, el_ref, er_ref, elat_ref, p_ref, pl_ref, pr_ref, plat_ref,
    xh_ref, xl_ref, la_ref, ba_ref, klt_ref, permt_ref, out_ref,
):
    rows = c_ref.shape[1]
    lanes = c_ref.shape[2]
    count = c_ref.shape[0]
    levels = el_ref.shape[1] // 2
    cols = rows // levels
    row_id = lax.broadcasted_iota(jnp.int32, (levels, cols, lanes), 1)
    plat = jnp.concatenate([plat_ref[...]] * count, axis=0)
    plane = (elat_ref[...].astype(F32) * plat).astype(BF)
    halo = nn(plane, xh_ref[...]) + nn(plane, xl_ref[...])
    for pair in range(count // 2):
        m0 = 2 * pair
        side = []
        for i in range(2):
            side.append(
                jnp.concatenate(
                    [
                        (er_ref[m0 + i].astype(F32) * pr_ref[...]).astype(BF),
                        (el_ref[m0 + i].astype(F32) * pl_ref[...]).astype(BF),
                    ],
                    axis=0,
                )
            )
        placed = nn(permt_ref[...], jnp.concatenate(side, axis=1))
        spread = []
        for i in range(2):
            own = (e_ref[m0 + i].astype(F32) * p_ref[...]).astype(BF).astype(F32)
            own = own.reshape(levels, cols, lanes)
            far = placed[:, i * lanes : (i + 1) * lanes].reshape(levels, cols, lanes)
            col = own
            for t in range(4):
                o = OFFSETS[t]
                from_far = (row_id >= cols - o) if o > 0 else (row_id < -o)
                col = col + taps_ref[4 + t] * pltpu.roll(jnp.where(from_far, far, own), o % cols, 1)
            y = nn(col.reshape(rows, lanes).astype(BF), la_ref[...])
            edge = tn(halo[8 * (m0 + i) : 8 * (m0 + i) + 8].astype(BF), ba_ref[...])
            spread.append((y[:, :lanes] + y[:, lanes:] + edge).astype(BF))
        back = nn(klt_ref[...], jnp.concatenate(spread, axis=1))
        for i in range(2):
            out_ref[m0 + i] = c_ref[m0 + i].astype(F32) + back[:, i * lanes : (i + 1) * lanes]


def full(shape):
    return pl.BlockSpec(shape, lambda g: (0,) * len(shape))


def shift(x, axis, step, wrap):
    n = lax.axis_size(axis)
    if step > 0:
        pairs = [(i, (i + 1) % n) for i in range(n if wrap else n - 1)]
    else:
        pairs = [((i + 1) % n, i) for i in range(n if wrap else n - 1)]
    return lax.ppermute(x, axis, pairs)


def shards(
    control, ensemble, level_mix, lat_taps, lon_taps, obs_location, obs_count, obs_keep, innovation, obs_weight
):
    members, levels, cols, lanes = control.shape
    rows = levels * cols
    half = 2 * levels
    ext = rows + 2 * half
    block = 8 if members % 8 == 0 else 2
    steps = members // block
    c3 = control.reshape(members, rows, lanes)
    e3 = ensemble.reshape(members, rows, lanes)
    params = pltpu.CompilerParams(vmem_limit_bytes=VMEM_LIMIT)

    smem = pl.BlockSpec(memory_space=pltpu.SMEM)
    own = np.arange(rows)
    own_level, own_col = own // cols, own % cols
    h = np.arange(half)
    ext_level = np.concatenate([own_level, h // 2, h // 2])
    ext_col = np.concatenate([own_col, h % 2 - 2, cols + h % 2])
    same_level = ext_level[:, None] == own_level[None, :]
    xcode = np.where(same_level, code_of(own_col[None, :] - ext_col[:, None]), 0).astype(np.int32)
    lane_id = np.arange(lanes)
    lat_code = code_of(lane_id[:, None] - lane_id[None, :])
    edge_pos = np.array([-2, -1, lanes, lanes + 1] * 2)
    e_code = code_of(edge_pos[:, None] - lane_id[None, :])
    e_code_t = code_of(lane_id[None, :] - edge_pos[:, None])
    spread_levels = (own_level[:, None] == np.arange(levels)[None, :]).astype(np.float32)
    same_col = (own_col[:, None] == own_col[None, :]).astype(np.float32)
    sel_lane = np.array([0, 1, lanes - 2, lanes - 1, -1, -1, -1, -1])
    sel = jnp.asarray((sel_lane[:, None] == lane_id[None, :]).astype(np.float32).astype(BF))
    pick_level = np.concatenate([h // 2, h // 2])
    pick_col = np.concatenate([h % 2, cols - 2 + h % 2])
    perm_np = ((pick_level * cols + pick_col)[:, None] == own[None, :]).astype(np.float32)
    perm = jnp.asarray(perm_np.astype(BF))
    perm_t = jnp.asarray(perm_np.T.astype(BF))
    taps = jnp.concatenate([lat_taps, lon_taps])

    member_block = lambda a, b: pl.BlockSpec((block, a, b), lambda g: (g, 0, 0))
    low, high = pl.pallas_call(
        column_kernel,
        grid=(steps,),
        in_specs=[member_block(rows, lanes), full((2 * half, rows))],
        out_specs=[member_block(half, lanes)] * 2,
        out_shape=[jax.ShapeDtypeStruct((members, half, lanes), BF)] * 2,
        compiler_params=params,
        cost_estimate=pl.CostEstimate(flops=10**9, bytes_accessed=8 * 10**6, transcendentals=0),
    )(e3, perm)
    e_left = shift(high, "lon", 1, True)
    e_right = shift(low, "lon", -1, True)

    ce, ee = pl.pallas_call(
        edge_kernel,
        grid=(steps,),
        in_specs=[member_block(rows, lanes)] * 2 + [full((8, lanes))],
        out_specs=[member_block(8, rows)] * 2,
        out_shape=[jax.ShapeDtypeStruct((members, 8, rows), BF)] * 2,
        compiler_params=params,
        cost_estimate=pl.CostEstimate(flops=10**9, bytes_accessed=11 * 10**6, transcendentals=0),
    )(c3, e3, sel)
    vm = pl.BlockSpec(memory_space=pltpu.VMEM)
    lf, la, bf, ba, lon_hi, lon_lo, kl, klt = pl.pallas_call(
        lambda *refs: setup_kernel(*refs[:8], *refs[9:], refs[8]),
        in_specs=[smem] + [vm] * 8,
        out_specs=[vm] * 8,
        out_shape=[jax.ShapeDtypeStruct(shape, BF) for shape in (
            (lanes, 2 * lanes), (lanes, 2 * lanes), (8, lanes), (8, lanes),
            (ext, rows), (ext, rows), (rows, rows), (rows, rows))],
        compiler_params=params,
        name="setup",
    )(taps, level_mix, jnp.asarray(lat_code), jnp.asarray(lat_code.T.copy()), jnp.asarray(e_code),
      jnp.asarray(e_code_t), jnp.asarray(spread_levels.astype(BF)), jnp.asarray(same_col.astype(BF)),
      jnp.asarray(xcode))

    both = jnp.concatenate([ce, ee], axis=0)
    before = shift(both[:, 2:4], "lat", 1, False)
    after = shift(both[:, 0:2], "lat", -1, False)
    lat_halo = jnp.concatenate([before, after], axis=1)
    lat_halo = jnp.concatenate([lat_halo, lat_halo], axis=1)
    ch, eh = lat_halo[:members], lat_halo[members:]
    corner = nt(eh.reshape(members * 8, rows), perm).astype(BF).reshape(members, 8, 2 * half)
    x_left = shift(corner[:, :4, half:], "lon", 1, True)
    x_right = shift(corner[:, :4, :half], "lon", -1, True)
    x_both = jnp.concatenate([x_left, x_right], axis=2)
    elat = jnp.concatenate([eh, jnp.concatenate([x_both, x_both], axis=1)], axis=2).reshape(members * 8, ext)

    inc, left, right = pl.pallas_call(
        forward_kernel,
        grid=(steps,),
        in_specs=[smem]
        + [member_block(rows, lanes)] * 2
        + [pl.BlockSpec((block * 8, rows), lambda g: (g, 0)), full((rows, rows)), full((rows, rows))]
        + [full((lanes, 2 * lanes)), full((8, lanes)), full((2 * half, rows))],
        out_specs=[full((rows, lanes))] + [member_block(half, lanes)] * 2,
        out_shape=[jax.ShapeDtypeStruct((rows, lanes), F32)]
        + [jax.ShapeDtypeStruct((members, half, lanes), BF)] * 2,
        compiler_params=params,
        cost_estimate=pl.CostEstimate(flops=10**10, bytes_accessed=20 * 10**6, transcendentals=0),
    )(taps, c3, e3, ch.reshape(members * 8, rows), kl, klt, lf, bf, perm)

    places = obs_location[0, 0]
    slots = places.shape[0]
    slot_ids = jnp.arange(slots, dtype=jnp.int32)
    live = (slot_ids < obs_count[0, 0]).astype(F32) * obs_keep[0, 0].astype(F32)
    q = live * obs_weight[0, 0]
    columns = ensemble.reshape(members, -1)[:, places]
    scaled = columns.astype(F32) * jnp.sqrt(q)[None, :]
    local_gram = jnp.dot(scaled, scaled.T, precision=lax.Precision.HIGHEST)
    local_gram, inc, left, right = lax.optimization_barrier((local_gram, inc, left, right))
    total_obs = slots * lax.axis_size("lat") * lax.axis_size("lon")
    gram = lax.psum(local_gram, ("lat", "lon"))
    upper = jnp.linalg.cholesky(jnp.eye(members, dtype=F32) + members / total_obs * gram).T

    to_left = jnp.sum(e_left.astype(F32) * left.astype(F32), axis=0)
    to_right = jnp.sum(e_right.astype(F32) * right.astype(F32), axis=0)
    from_right = shift(to_left, "lon", -1, True)
    from_left = shift(to_right, "lon", 1, True)
    cube = inc.reshape(levels, cols, lanes)
    zeros = jnp.zeros((levels, cols - 2, lanes), F32)
    cube = (
        cube
        + jnp.concatenate([from_left.reshape(levels, 2, lanes), zeros], axis=1)
        + jnp.concatenate([zeros, from_right.reshape(levels, 2, lanes)], axis=1)
    )

    pulled, p_edge = pl.pallas_call(
        obs_kernel,
        out_shape=[jax.ShapeDtypeStruct((rows, lanes), F32), jax.ShapeDtypeStruct((8, rows), F32)],
        compiler_params=params,
    )(cube.reshape(rows, lanes), places[None], q[None], innovation[0])

    p_before = shift(p_edge[2:4], "lat", 1, False)
    p_after = shift(p_edge[0:2], "lat", -1, False)
    plat = jnp.concatenate([p_before, p_after], axis=0)
    plat3 = plat.reshape(4, levels, cols)
    p3 = pulled.reshape(levels, cols, lanes)
    def packed(piece, corner):
        wide = jnp.pad(corner.reshape(4, half), ((0, 4), (0, lanes - half)))
        return jnp.concatenate([piece.reshape(half, lanes), wide], axis=0)

    p_left = shift(packed(p3[:, cols - 2 :], plat3[:, :, cols - 2 :]), "lon", 1, True)
    p_right = shift(packed(p3[:, :2], plat3[:, :, :2]), "lon", -1, True)
    px_left, px_right = p_left[half : half + 4, :half], p_right[half : half + 4, :half]
    p_left, p_right = p_left[:half], p_right[:half]
    plat = jnp.concatenate([plat, px_left, px_right], axis=1)
    plat = jnp.concatenate([plat, plat], axis=0)

    gradient = pl.pallas_call(
        adjoint_kernel,
        grid=(steps,),
        in_specs=[smem]
        + [member_block(rows, lanes)] * 2
        + [member_block(half, lanes)] * 2
        + [pl.BlockSpec((block * 8, ext), lambda g: (g, 0))]
        + [full((rows, lanes)), full((half, lanes)), full((half, lanes)), full((8, ext))]
        + [full((ext, rows))] * 2
        + [full((lanes, 2 * lanes)), full((8, lanes)), full((rows, rows)), full((rows, 2 * half))],
        out_specs=member_block(rows, lanes),
        out_shape=jax.ShapeDtypeStruct((members, rows, lanes), F32),
        compiler_params=params,
        cost_estimate=pl.CostEstimate(flops=10**10, bytes_accessed=24 * 10**6, transcendentals=0),
    )(taps, c3, e3, e_left, e_right, elat, pulled, p_left, p_right, plat,
      lon_hi, lon_lo, la, ba, klt, perm_t)
    return gradient.reshape(members, levels, cols, lanes), upper


def solution(mesh):
    in_specs = (
        P(None, None, "lon", "lat"),
        P(None, None, "lon", "lat"),
        P(),
        P(),
        P(),
        P("lon", "lat", None),
        P("lon", "lat"),
        P("lon", "lat", None),
        P("lon", "lat", None),
        P("lon", "lat", None),
    )
    out_specs = (P(None, None, "lon", "lat"), P())
    return jax.shard_map(shards, mesh=mesh, in_specs=in_specs, out_specs=out_specs, check_vma=False)
```

time: 212 us -> 192 us (0.906)
  other arithmetic: 39.9 us -> 17.9 us
  Pallas kernels: 61.6 us -> 66.6 us
  starting transfers between devices: 32.5 us -> 29.2 us
  waiting for transfers between devices: 1.98 us -> 4.69 us
    convert_element_type x7 -> x0, other arithmetic: 17 us -> none  [the longest x5 15.7 us: split2(): return (hi.astype(BF), (x - hi).astype(BF))]
    pallas_call x2 -> x4, Pallas kernels: 46.8 us -> 52.9 us  [the longest x1 21.6 us: shards(): pl.pallas_call(forward_kernel, grid=(steps,), in_specs=[smem] + [member_b...]
    ppermute x14 -> x12, starting transfers between devices: 32.5 us -> 29.2 us  [shift(): return lax.ppermute(x, axis, pairs)]
    ppermute x14 -> x12, waiting for transfers between devices: 1.98 us -> 4.69 us  [shift(): return lax.ppermute(x, axis, pairs)]
    concatenate x6 -> x3, other arithmetic: 3.39 us -> 0.68 us  [the longest x1 0.67 us: shards(): taps = jnp.concatenate([lat_taps, lon_taps])]
    unnamed x36 -> x20, local copies, waits for them, and re-layouts: 12.9 us -> 11.7 us
  transfers between devices with their start and end apart: 14 -> 12, of which waited for: 2 -> 2; matrix products, arithmetic and copies ran while one was open for 33% -> 24% of each run, Pallas kernels for 12% -> 19%
where the time goes in v2:
time: 192 us; the launch traced here: 191 us
  Pallas kernels  66.6 us (35%)
  blocking collectives  39.9 us (21%)
  starting transfers between devices  29.2 us (15%)
  local copies, waits for them, and re-layouts  28 us (15%)
  other arithmetic  17.9 us (9%)
  waiting for transfers between devices  4.69 us (2%)
  matrix products  2.63 us (1%)
    psum x1, blocking collectives, shards(): gram = lax.psum(local_gram, ('lat', 'lon'))  39.9 us
    ppermute x12, starting transfers between devices, shift(): return lax.ppermute(x, axis, pairs)  29.2 us
    pallas_call x1, Pallas kernels, shards(): pl.pallas_call(forward_kernel, grid=(steps,), in_specs=[smem] + [member_b...  21.6 us
    pallas_call x1, Pallas kernels, shards(): pl.pallas_call(adjoint_kernel, grid=(steps,), in_specs=[smem] + [member_b...  20.3 us
    unnamed x20, local copies, waits for them, and re-layouts  11.7 us
    gather x1, local copies, waits for them, and re-layouts, shards(): columns = ensemble.reshape(members, -1)[:, places]  10.1 us
    pallas_call x1, Pallas kernels, shards(): pl.pallas_call(edge_kernel, grid=(steps,), in_specs=[member_block(rows, l...  9.58 us
    pallas_call x1, Pallas kernels, shards(): pl.pallas_call(column_kernel, grid=(steps,), in_specs=[member_block(rows,...  8.19 us
  transfers between devices with their start and end apart: 12, of which 2 were waited for; matrix products, arithmetic and copies ran while one was open for 24% of the time, Pallas kernels for 19%

profile of v2, /device:TPU:1, one launch (start us, length us, event | category | flops | bytes accessed | tf_op | source)
XLA Modules:
  0.0 190.5 jit_solution(7862433003233347181)
XLA Ops:
  0.6 9.6 %shard_map.204 = (bf16[80,8,256]{2,1,0:T(8,128)(2,1)}, bf16[80,8,256]{2,1,0:T(8,128)(2,1)}) custom-call(bf16[80,256,128]{2,1,0:T(8,128)(2,1)} %bitcast.54, bf16[80,256,128]{2,1,0:T(8,128)(2,1)} %bitcast.49, bf16[8,128]{1,0:T(8,128)(2,1)} %constant.68.clone.sel_ref), custom_call_target="tpu_custom_call" | custom-call | flops 1000000000 | bytes 11000000 | tf_op jit(solution)/shard_map/pallas_call | solution.py:274
  10.2 1.0 constant_dynamic-update-slice_fusion.1
  11.2 1.0 constant_dynamic-update-slice_fusion
  12.4 4.5 %collective-permute-start.2 = (bf16[160,2,256]{2,1,0:T(2,128)(2,1)S(1)}, bf16[160,2,256]{2,1,0:T(2,128)(2,1)S(1)}, u32[]{:S(2)}, u32[]{:S(2)}) collective-permute-start(bf16[160,2,256]{2,1,0:T(2,128)(2,1)S(1)} %get-tuple-element.46), channel_id=1, source_target_pairs={{0,8},{8,16},{16,24},{1,9},{9,17},{17,25},{2,10},{10,18},{18,26},{... | collective-permute-start | bytes 491528 | tf_op jit(solution)/shard_map/ppermute | solution.py:221
  17.0 1.9 %collective-permute-start.3 = (bf16[160,2,256]{2,1,0:T(2,128)(2,1)S(1)}, bf16[160,2,256]{2,1,0:T(2,128)(2,1)S(1)}, u32[]{:S(2)}, u32[]{:S(2)}) collective-permute-start(bf16[160,2,256]{2,1,0:T(2,128)(2,1)S(1)} %get-tuple-element.47), channel_id=1, source_target_pairs={{8,0},{16,8},{24,16},{9,1},{17,9},{25,17},{10,2},{18,10},{26,18},{... | collective-permute-start | bytes 491528 | tf_op jit(solution)/shard_map/ppermute | solution.py:221
  18.9 8.2 %shard_map.203 = (bf16[80,64,128]{2,1,0:T(8,128)(2,1)}, bf16[80,64,128]{2,1,0:T(8,128)(2,1)}) custom-call(bf16[80,256,128]{2,1,0:T(8,128)(2,1)} %bitcast.50, bf16[128,256]{1,0:T(8,128)(2,1)} %constant.69.clone.perm_ref), custom_call_target="tpu_custom_call" | custom-call | flops 1000000000 | bytes 8000000 | tf_op jit(solution)/shard_map/pallas_call | solution.py:262
  27.1 4.2 %collective-permute-start.1 = (bf16[80,64,128]{2,1,0:T(8,128)(2,1)}, bf16[80,64,128]{2,1,0:T(8,128)(2,1)S(1)}, u32[]{:S(2)}, u32[]{:S(2)}) collective-permute-start(bf16[80,64,128]{2,1,0:T(8,128)(2,1)} %get-tuple-element.24), channel_id=1, source_target_pairs={{1,0},{2,1},{3,2},{4,3},{5,4},{6,5},{7,6},{0,7},{9,8},{10,9},{11,1... | collective-permute-start | bytes 3932168 | tf_op jit(solution)/shard_map/ppermute | solution.py:221
  31.4 10.6 %copy.27 = bf16[80,32,8,128]{0,3,2,1:T(8,128)(2,1)} copy(bf16[80,32,8,128]{3,2,1,0:T(8,128)(2,1)} %param.21) | data formatting | bytes 10485760 | tf_op args[1]
  43.5 10.1 %gather_fusion = bf16[2048,80]{1,0:T(8,128)(2,1)S(1)} fusion(bf16[80,32768]{0,1:T(8,128)(2,1)} %bitcast.53, s32[2048]{0:T(1024)S(1)} %broadcast_clamp_fusion), kind=kCustom, calls=%fused_computation | custom fusion | bytes 663552 | tf_op jit(solution)/shard_map/gather | solution.py:328
  54.2 2.8 %setup.1 = (bf16[128,256]{1,0:T(8,128)(2,1)}, bf16[128,256]{1,0:T(8,128)(2,1)}, bf16[8,128]{1,0:T(8,128)(2,1)}, bf16[8,128]{1,0:T(8,128)(2,1)}, bf16[384,256]{1,...) custom-call(f32[8]{0:T(128)} %pad_maximum_fusion.2.refs_0_.taps_ref, ...), custom_call_target="tpu_custom_call" | custom-call | tf_op jit(solution)/shard_map/setup/pallas_call | solution.py:284
  57.0 2.4 %fusion.1 = f32[80,80]{1,0:T(8,128)S(1)} fusion(bf16[2048,80]{1,0:T(8,128)(2,1)S(1)} %gather_fusion, f32[2048]{0:T(1024)S(1)} %multiply_sqrt_fusion), kind=kOutput, calls=%fused_computation.5 | convolution fusion | flops 157614080 | bytes 361472 | tf_op jit(solution)/shard_map/dot_general | solution.py:330
  60.0 0.8 slice_bitcast_fusion
  60.8 21.6 %shard_map.205 = (f32[256,128]{1,0:T(8,128)}, bf16[80,64,128]{2,1,0:T(8,128)(2,1)}, bf16[80,64,128]{2,1,0:T(8,128)(2,1)}) custom-call(f32[8]{0:T(128)} %pad_maximum_fusion.2.refs_0_.taps_ref, bf16[80,256,128]{2,1,0:T(8,128)(2,1)} %bitcast.55, bf16[80,256,128]{2,1,0:T(8,128)(2,1)} %bitcast.51, bf16[640,256]{1,0:T(8,128)(2,1)} %get-tuple-element.44.ch_ref, ...), custom_call_target="tpu_custom_call" | custom-call | flops 10000000000 | bytes 20000000 | tf_op jit(solution)/shard_map/pallas_call | solution.py:309
  82.5 39.9 %psum.7 = f32[80,80]{0,1:T(8,128)S(1)} all-reduce(f32[80,80]{0,1:T(8,128)S(1)} %copy.32), channel_id=1, replica_groups=mesh['lat'=4,'lon'=8] {'lat','lon'}, use_global_device_ids=true, to_apply=%region_2.3 | all-reduce | flops 6400 | bytes 51200 | tf_op jit(solution)/shard_map/psum | solution.py:333
  122.5 7.3 %cholesky.20 = f32[80,80]{1,0:T(8,128)S(1)} custom-call(f32[80,80]{1,0:T(8,128)S(1)} %fusion.8), custom_call_target="Cholesky" | custom-call | tf_op jit(solution)/shard_map/jit(cholesky)/cholesky | solution.py:334
  130.0 0.7 compare_reduce_fusion
  131.1 2.3 %multiply_reduce_fusion.1 = f32[64,128]{1,0:T(8,128)S(1)} fusion(bf16[80,64,128]{2,1,0:T(8,128)(2,1)} %get-tuple-element.35, bf16[80,64,128]{2,1,0:T(8,128)(2,1)S(1)} %collective-permute-done.1.er_ref), kind=kLoop, calls=%fused_computation.2 | loop fusion | flops 2613248 | bytes 2654208 | tf_op jit(solution)/shard_map/reduce_sum | solution.py:337
  133.5 0.8 collective-permute-start.6
  134.3 1.8 multiply_reduce_fusion
  136.1 3.7 %collective-permute-start.7 = (f32[64,128]{1,0:T(8,128)S(1)}, f32[64,128]{1,0:T(8,128)S(1)}, u32[]{:S(2)}, u32[]{:S(2)}) collective-permute-start(f32[64,128]{1,0:T(8,128)S(1)} %multiply_reduce_fusion), channel_id=1, source_target_pairs={{1,0},{2,1},{3,2},{4,3},{5,4},{6,5},{7,6},{0,7},{9,8},{10,9},{11,1... | collective-permute-start | bytes 98312 | tf_op jit(solution)/shard_map/ppermute | solution.py:221
  139.8 1.3 select_bitcast_fusion
  141.0 4.2 %collective-permute-start.5 = (bf16[80,4,64]{2,1,0:T(4,128)(2,1)S(1)}, bf16[80,4,64]{2,1,0:T(4,128)(2,1)S(1)}, u32[]{:S(2)}, u32[]{:S(2)}) collective-permute-start(bf16[80,4,64]{2,1,0:T(4,128)(2,1)S(1)} %get-tuple-element.49), channel_id=1, source_target_pairs={{1,0},{2,1},{3,2},{4,3},{5,4},{6,5},{7,6},{0,7},{9,8},{10,9},{11,1... | collective-permute-start | bytes 122888 | tf_op jit(solution)/shard_map/ppermute | solution.py:221
  145.9 4.1 %shard_map.206 = (f32[256,128]{1,0:T(8,128)}, f32[8,256]{1,0:T(8,128)}) custom-call(f32[256,128]{1,0:T(8,128)} %fusion.7.inc_ref, s32[1,2048]{1,0:T(1,128)} %bitcast.64, f32[1,2048]{1,0:T(1,128)} %fusion.9.q_ref, f32[1,2048]{1,0:T(1,128)} %bitcast.68), custom_call_target="tpu_custom_call" | custom-call | tf_op jit(solution)/shard_map/pallas_call | solution.py:348
  150.0 0.8 fusion.15
  150.8 6.3 %collective-permute-start.8 = (f32[2,256]{1,0:T(2,128)S(1)}, f32[2,256]{1,0:T(2,128)S(1)}, u32[]{:S(2)}, u32[]{:S(2)}) collective-permute-start(f32[2,256]{1,0:T(2,128)S(1)} %get-tuple-element.54), channel_id=1, source_target_pairs={{0,8},{8,16},{16,24},{1,9},{9,17},{17,25},{2,10},{10,18},{18,26},{... | collective-permute-start | bytes 6152 | tf_op jit(solution)/shard_map/ppermute | solution.py:221
  157.1 1.9 %collective-permute-start.9 = (f32[2,256]{1,0:T(2,128)S(1)}, f32[2,256]{1,0:T(2,128)S(1)}, u32[]{:S(2)}, u32[]{:S(2)}) collective-permute-start(f32[2,256]{1,0:T(2,128)S(1)} %get-tuple-element.55), channel_id=1, source_target_pairs={{8,0},{16,8},{24,16},{9,1},{17,9},{25,17},{10,2},{18,10},{26,18},{... | collective-permute-start | bytes 6152 | tf_op jit(solution)/shard_map/ppermute | solution.py:221
  159.1 1.0 fusion.13
  160.1 2.0 %collective-permute-done.9 = f32[2,256]{1,0:T(2,128)S(1)} collective-permute-done((f32[2,256]{1,0:T(2,128)S(1)}, f32[2,256]{1,0:T(2,128)S(1)}, u32[]{:S(2)}, u32[]{:S(2)}) %collective-permute-start.9) | collective-permute-done | bytes 2080 | tf_op jit(solution)/shard_map/ppermute | solution.py:221
  163.4 1.2 collective-permute-start.10
  164.6 1.1 maximum_bitcast_fusion.elat_ref
  166.3 2.7 %collective-permute-done.10 = f32[72,128]{1,0:T(8,128)S(1)} collective-permute-done((f32[72,128]{1,0:T(8,128)S(1)}, f32[72,128]{1,0:T(8,128)S(1)}, u32[]{:S(2)}, u32[]{:S(2)}) %collective-permute-start.10) | collective-permute-done | bytes 36896 | tf_op jit(solution)/shard_map/ppermute | solution.py:221
  170.3 20.3 %shard_map.207 = f32[80,256,128]{2,1,0:T(8,128)} custom-call(f32[8]{0:T(128)} %pad_maximum_fusion.2.refs_0_.taps_ref, bf16[80,256,128]{2,1,0:T(8,128)(2,1)} %bitcast.56, bf16[80,256,128]{2,1,0:T(8,128)(2,1)} %bitcast.52, bf16[80,64,128]{2,1,0:T(8,128)(2,1)} %collective-permute-done.el_ref, bf16[80,64,128]{2,1,0:T(8,128)(2,1)} %copy-done, ...), custom_call_target="tpu_custom_call" | custom-call | flops 10000000000 | bytes 24000000 | tf_op jit(solution)/shard_map/pallas_call | solution.py:370
  (62 shorter events, 6.9 us)
Async XLA Ops:
  12.4 46.9 %collective-permute-start.2 = (bf16[160,2,256]{2,1,0:T(2,128)(2,1)S(1)}, bf16[160,2,256]{2,1,0:T(2,128)(2,1)S(1)}, u32[]{:S(2)}, u32[]{:S(2)}) collective-permute-start(bf16[160,2,256]{2,1,0:T(2,128)(2,1)S(1)} %get-tuple-element.46), channel_id=1, source_target_pairs={{0,8},{8,16},{16,24},{1,9},{9,17},{17,25},{2,10},{10,18},{18,26},{... | collective-permute-start | bytes 491528 | tf_op jit(solution)/shard_map/ppermute | solution.py:221
  17.0 42.4 %collective-permute-start.3 = (bf16[160,2,256]{2,1,0:T(2,128)(2,1)S(1)}, bf16[160,2,256]{2,1,0:T(2,128)(2,1)S(1)}, u32[]{:S(2)}, u32[]{:S(2)}) collective-permute-start(bf16[160,2,256]{2,1,0:T(2,128)(2,1)S(1)} %get-tuple-element.47), channel_id=1, source_target_pairs={{8,0},{16,8},{24,16},{9,1},{17,9},{25,17},{10,2},{18,10},{26,18},{... | collective-permute-start | bytes 491528 | tf_op jit(solution)/shard_map/ppermute | solution.py:221
  27.1 104.0 %collective-permute-start.1 = (bf16[80,64,128]{2,1,0:T(8,128)(2,1)}, bf16[80,64,128]{2,1,0:T(8,128)(2,1)S(1)}, u32[]{:S(2)}, u32[]{:S(2)}) collective-permute-start(bf16[80,64,128]{2,1,0:T(8,128)(2,1)} %get-tuple-element.24), channel_id=1, source_target_pairs={{1,0},{2,1},{3,2},{4,3},{5,4},{6,5},{7,6},{0,7},{9,8},{10,9},{11,1... | collective-permute-start | bytes 3932168 | tf_op jit(solution)/shard_map/ppermute | solution.py:221
  31.3 11.4 %copy-start.5 = (s32[1,1,2048]{2,1,0:T(1,128)S(1)}, s32[1,1,2048]{2,1,0:T(1,128)}, u32[]{:S(2)}) copy-start(s32[1,1,2048]{2,1,0:T(1,128)} %param.27) | copy-start | bytes 24580
  31.3 11.4 %copy-start.6 = (s32[1,1,2048]{2,1,0:T(1,128)S(1)}, s32[1,1,2048]{2,1,0:T(1,128)}, u32[]{:S(2)}) copy-start(s32[1,1,2048]{2,1,0:T(1,128)} %param.25) | copy-start | bytes 24580
  31.3 11.4 %copy-start.7 = (f32[4]{0:T(128)S(1)}, f32[4]{0:T(128)}, u32[]{:S(2)}) copy-start(f32[4]{0:T(128)} %param.24) | copy-start | bytes 52
  31.3 11.4 %copy-start.8 = (f32[4]{0:T(128)S(1)}, f32[4]{0:T(128)}, u32[]{:S(2)}) copy-start(f32[4]{0:T(128)} %param.23) | copy-start | bytes 52
  31.3 102.9 %collective-permute-start = (bf16[80,64,128]{2,1,0:T(8,128)(2,1)}, bf16[80,64,128]{2,1,0:T(8,128)(2,1)}, u32[]{:S(2)}, u32[]{:S(2)}) collective-permute-start(bf16[80,64,128]{2,1,0:T(8,128)(2,1)} %get-tuple-element.23), channel_id=1, source_target_pairs={{0,1},{1,2},{2,3},{3,4},{4,5},{5,6},{6,7},{7,0},{8,9},{9,10},{10,1... | collective-permute-start | bytes 3932168 | tf_op jit(solution)/shard_map/ppermute | solution.py:221
  43.4 10.1 %copy-start.4 = (f32[1,1,2048]{2,1,0:T(1,128)S(1)}, f32[1,1,2048]{2,1,0:T(1,128)}, u32[]{:S(2)}) copy-start(f32[1,1,2048]{2,1,0:T(1,128)} %param.29) | copy-start | bytes 24580
  60.8 69.9 %copy-start.2 = (bf16[128,256]{1,0:T(8,128)(2,1)S(1)}, bf16[128,256]{1,0:T(8,128)(2,1)}, u32[]{:S(2)}) copy-start(bf16[128,256]{1,0:T(8,128)(2,1)} %constant.69.clone.perm_ref) | copy-start | bytes 196612
  131.1 3.2 %copy-start.1 = (bf16[80,64,128]{2,1,0:T(8,128)(2,1)S(1)}, bf16[80,64,128]{2,1,0:T(8,128)(2,1)}, u32[]{:S(2)}) copy-start(bf16[80,64,128]{2,1,0:T(8,128)(2,1)} %get-tuple-element.36) | copy-start | bytes 3932164
  131.1 2.3 %copy-start = (bf16[80,64,128]{2,1,0:T(8,128)(2,1)}, bf16[80,64,128]{2,1,0:T(8,128)(2,1)S(1)}, u32[]{:S(2)}) copy-start(bf16[80,64,128]{2,1,0:T(8,128)(2,1)S(1)} %collective-permute-done.1.er_ref) | copy-start | bytes 3932164
  133.5 11.7 %copy-start.3 = (f32[256,128]{1,0:T(8,128)S(1)}, f32[256,128]{1,0:T(8,128)}, u32[]{:S(2)}) copy-start(f32[256,128]{1,0:T(8,128)} %get-tuple-element.34) | copy-start | bytes 393220
  133.5 11.7 %collective-permute-start.6 = (f32[64,128]{1,0:T(8,128)S(1)}, f32[64,128]{1,0:T(8,128)S(1)}, u32[]{:S(2)}, u32[]{:S(2)}) collective-permute-start(f32[64,128]{1,0:T(8,128)S(1)} %multiply_reduce_fusion.1), channel_id=1, source_target_pairs={{0,1},{1,2},{2,3},{3,4},{4,5},{5,6},{6,7},{7,0},{8,9},{9,10},{10,1... | collective-permute-start | bytes 98312 | tf_op jit(solution)/shard_map/ppermute | solution.py:221
  136.1 9.1 %collective-permute-start.7 = (f32[64,128]{1,0:T(8,128)S(1)}, f32[64,128]{1,0:T(8,128)S(1)}, u32[]{:S(2)}, u32[]{:S(2)}) collective-permute-start(f32[64,128]{1,0:T(8,128)S(1)} %multiply_reduce_fusion), channel_id=1, source_target_pairs={{1,0},{2,1},{3,2},{4,3},{5,4},{6,5},{7,6},{0,7},{9,8},{10,9},{11,1... | collective-permute-start | bytes 98312 | tf_op jit(solution)/shard_map/ppermute | solution.py:221
  141.0 23.6 %collective-permute-start.4 = (bf16[80,4,64]{2,1,0:T(4,128)(2,1)S(1)}, bf16[80,4,64]{2,1,0:T(4,128)(2,1)S(1)}, u32[]{:S(2)}, u32[]{:S(2)}) collective-permute-start(bf16[80,4,64]{2,1,0:T(4,128)(2,1)S(1)} %get-tuple-element.48), channel_id=1, source_target_pairs={{0,1},{1,2},{2,3},{3,4},{4,5},{5,6},{6,7},{7,0},{8,9},{9,10},{10,1... | collective-permute-start | bytes 122888 | tf_op jit(solution)/shard_map/ppermute | solution.py:221
  141.0 23.6 %collective-permute-start.5 = (bf16[80,4,64]{2,1,0:T(4,128)(2,1)S(1)}, bf16[80,4,64]{2,1,0:T(4,128)(2,1)S(1)}, u32[]{:S(2)}, u32[]{:S(2)}) collective-permute-start(bf16[80,4,64]{2,1,0:T(4,128)(2,1)S(1)} %get-tuple-element.49), channel_id=1, source_target_pairs={{1,0},{2,1},{3,2},{4,3},{5,4},{6,5},{7,6},{0,7},{9,8},{10,9},{11,1... | collective-permute-start | bytes 122888 | tf_op jit(solution)/shard_map/ppermute | solution.py:221
  150.8 9.3 %collective-permute-start.8 = (f32[2,256]{1,0:T(2,128)S(1)}, f32[2,256]{1,0:T(2,128)S(1)}, u32[]{:S(2)}, u32[]{:S(2)}) collective-permute-start(f32[2,256]{1,0:T(2,128)S(1)} %get-tuple-element.54), channel_id=1, source_target_pairs={{0,8},{8,16},{16,24},{1,9},{9,17},{17,25},{2,10},{10,18},{18,26},{... | collective-permute-start | bytes 6152 | tf_op jit(solution)/shard_map/ppermute | solution.py:221
  157.1 4.9 %collective-permute-start.9 = (f32[2,256]{1,0:T(2,128)S(1)}, f32[2,256]{1,0:T(2,128)S(1)}, u32[]{:S(2)}, u32[]{:S(2)}) collective-permute-start(f32[2,256]{1,0:T(2,128)S(1)} %get-tuple-element.55), channel_id=1, source_target_pairs={{8,0},{16,8},{24,16},{9,1},{17,9},{25,17},{10,2},{18,10},{26,18},{... | collective-permute-start | bytes 6152 | tf_op jit(solution)/shard_map/ppermute | solution.py:221
  162.6 3.0 %collective-permute-start.11 = (f32[72,128]{1,0:T(8,128)S(1)}, f32[72,128]{1,0:T(8,128)S(1)}, u32[]{:S(2)}, u32[]{:S(2)}) collective-permute-start(f32[72,128]{1,0:T(8,128)S(1)} %select_maximum_fusion), channel_id=1, source_target_pairs={{1,0},{2,1},{3,2},{4,3},{5,4},{6,5},{7,6},{0,7},{9,8},{10,9},{11,1... | collective-permute-start | bytes 110600 | tf_op jit(solution)/shard_map/ppermute | solution.py:221
  163.4 5.6 %collective-permute-start.10 = (f32[72,128]{1,0:T(8,128)S(1)}, f32[72,128]{1,0:T(8,128)S(1)}, u32[]{:S(2)}, u32[]{:S(2)}) collective-permute-start(f32[72,128]{1,0:T(8,128)S(1)} %select_maximum_fusion.1), channel_id=1, source_target_pairs={{0,1},{1,2},{2,3},{3,4},{4,5},{5,6},{6,7},{7,0},{8,9},{9,10},{10,1... | collective-permute-start | bytes 110600 | tf_op jit(solution)/shard_map/ppermute | solution.py:221

commit v3 on v2

--- a/solution.py
+++ b/solution.py
@@ -221,6 +221,17 @@
     return lax.ppermute(x, axis, pairs)
 
 
+def butterfly(x, axis):
+    n = lax.axis_size(axis)
+    if n & (n - 1):
+        return lax.psum(x, axis)
+    bit = 1
+    while bit < n:
+        x = x + lax.ppermute(x, axis, [(i, i ^ bit) for i in range(n)])
+        bit *= 2
+    return x
+
+
 def shards(
     control, ensemble, level_mix, lat_taps, lon_taps, obs_location, obs_count, obs_keep, innovation, obs_weight
 ):
@@ -268,9 +279,10 @@
         compiler_params=params,
         cost_estimate=pl.CostEstimate(flops=10**9, bytes_accessed=8 * 10**6, transcendentals=0),
     )(e3, perm)
-    e_left = shift(high, "lon", 1, True)
-    e_right = shift(low, "lon", -1, True)
-
+
+    sel, e_left_src, e_right_src = lax.optimization_barrier((sel, high, low))
+    e_left = shift(e_left_src, "lon", 1, True)
+    e_right = shift(e_right_src, "lon", -1, True)
     ce, ee = pl.pallas_call(
         edge_kernel,
         grid=(steps,),
@@ -328,9 +340,8 @@
     columns = ensemble.reshape(members, -1)[:, places]
     scaled = columns.astype(F32) * jnp.sqrt(q)[None, :]
     local_gram = jnp.dot(scaled, scaled.T, precision=lax.Precision.HIGHEST)
-    local_gram, inc, left, right = lax.optimization_barrier((local_gram, inc, left, right))
     total_obs = slots * lax.axis_size("lat") * lax.axis_size("lon")
-    gram = lax.psum(local_gram, ("lat", "lon"))
+    gram = butterfly(butterfly(local_gram, "lat"), "lon")
     upper = jnp.linalg.cholesky(jnp.eye(members, dtype=F32) + members / total_obs * gram).T
 
     to_left = jnp.sum(e_left.astype(F32) * left.astype(F32), axis=0)

time: 192 us -> 184 us (0.958)
  blocking collectives: 39.9 us -> 0 us
  waiting for transfers between devices: 4.69 us -> 33.7 us
  starting transfers between devices: 29.2 us -> 33 us
    psum x1 -> x0, blocking collectives: 39.9 us -> none  [shards(): gram = lax.psum(local_gram, ('lat', 'lon'))]
    ppermute x0 -> x5, waiting for transfers between devices: none -> 28 us  [butterfly(): x = x + lax.ppermute(x, axis, [(i, i ^ bit) for i in range(n)])]
    ppermute x0 -> x5, starting transfers between devices: none -> 5.94 us  [butterfly(): x = x + lax.ppermute(x, axis, [(i, i ^ bit) for i in range(n)])]
    ppermute x12, starting transfers between devices: 29.2 us -> 27 us  [shift(): return lax.ppermute(x, axis, pairs)]
    unnamed x20 -> x22, local copies, waits for them, and re-layouts: 11.7 us -> 12.2 us
  transfers between devices with their start and end apart: 12 -> 17, of which waited for: 2 -> 4; matrix products, arithmetic and copies ran while one was open for 24% -> 12% of each run, Pallas kernels for 19% -> 25%
where the time goes in v3:
time: 184 us; the launch traced here: 183 us
  Pallas kernels  66.6 us (36%)
  waiting for transfers between devices  33.7 us (18%)
  starting transfers between devices  33 us (18%)
  local copies, waits for them, and re-layouts  28.5 us (15%)
  other arithmetic  17.3 us (9%)
  matrix products  2.61 us (1%)
    ppermute x5, waiting for transfers between devices, butterfly(): x = x + lax.ppermute(x, axis, [(i, i ^ bit) for i in range(n)])  28 us
    ppermute x12, starting transfers between devices, shift(): return lax.ppermute(x, axis, pairs)  27 us
    pallas_call x1, Pallas kernels, shards(): pl.pallas_call(forward_kernel, grid=(steps,), in_specs=[smem] + [member_b...  21.6 us
    pallas_call x1, Pallas kernels, shards(): pl.pallas_call(adjoint_kernel, grid=(steps,), in_specs=[smem] + [member_b...  20.3 us
    unnamed x22, local copies, waits for them, and re-layouts  12.2 us
    gather x1, local copies, waits for them, and re-layouts, shards(): columns = ensemble.reshape(members, -1)[:, places]  10.1 us
    pallas_call x1, Pallas kernels, shards(): pl.pallas_call(edge_kernel, grid=(steps,), in_specs=[member_block(rows, l...  9.61 us
    pallas_call x1, Pallas kernels, shards(): pl.pallas_call(column_kernel, grid=(steps,), in_specs=[member_block(rows,...  8.18 us
  transfers between devices with their start and end apart: 17, of which 4 were waited for; matrix products, arithmetic and copies ran while one was open for 12% of the time, Pallas kernels for 25%

profile of v3, /device:TPU:1, one launch (start us, length us, event | category | flops | bytes accessed | tf_op | source)
XLA Modules:
  0.0 183.3 jit_solution(17678382549895658515)
XLA Ops:
  2.0 10.6 %copy.32 = bf16[80,32,8,128]{0,3,2,1:T(8,128)(2,1)} copy(bf16[80,32,8,128]{3,2,1,0:T(8,128)(2,1)} %param.21) | data formatting | bytes 10485760 | tf_op args[1]
  12.7 10.1 %gather_fusion = bf16[2048,80]{1,0:T(8,128)(2,1)S(1)} fusion(bf16[80,32768]{0,1:T(8,128)(2,1)} %bitcast.53, s32[2048]{0:T(1024)S(1)} %broadcast_clamp_fusion), kind=kCustom, calls=%fused_computation | custom fusion | bytes 663552 | tf_op jit(solution)/shard_map/gather | solution.py:340
  22.8 2.4 %fusion.1 = f32[80,80]{0,1:T(8,128)S(1)} fusion(bf16[2048,80]{1,0:T(8,128)(2,1)S(1)} %gather_fusion, f32[2048]{0:T(1024)S(1)} %multiply_sqrt_fusion), kind=kOutput, calls=%fused_computation.5 | convolution fusion | flops 157614080 | bytes 361472 | tf_op jit(solution)/shard_map/dot_general | solution.py:342
  25.2 8.2 %shard_map.203 = (bf16[80,64,128]{2,1,0:T(8,128)(2,1)}, bf16[80,64,128]{2,1,0:T(8,128)(2,1)}) custom-call(bf16[80,256,128]{2,1,0:T(8,128)(2,1)} %bitcast.49, bf16[128,256]{1,0:T(8,128)(2,1)} %constant.69.clone.perm_ref), custom_call_target="tpu_custom_call" | custom-call | flops 1000000000 | bytes 8000000 | tf_op jit(solution)/shard_map/pallas_call | solution.py:273
  33.4 9.6 %shard_map.204 = (bf16[80,8,256]{2,1,0:T(8,128)(2,1)}, bf16[80,8,256]{2,1,0:T(8,128)(2,1)}) custom-call(bf16[80,256,128]{2,1,0:T(8,128)(2,1)} %bitcast.54, bf16[80,256,128]{2,1,0:T(8,128)(2,1)} %bitcast.50, bf16[8,128]{1,0:T(8,128)(2,1)} %constant.68.clone.sel_ref), custom_call_target="tpu_custom_call" | custom-call | flops 1000000000 | bytes 11000000 | tf_op jit(solution)/shard_map/pallas_call | solution.py:286
  43.0 1.0 constant_dynamic-update-slice_fusion.1
  44.1 2.8 %collective-permute-start.13 = (f32[80,80]{0,1:T(8,128)S(1)}, f32[80,80]{0,1:T(8,128)S(1)}, u32[]{:S(2)}, u32[]{:S(2)}) collective-permute-start(f32[80,80]{0,1:T(8,128)S(1)} %add.58), channel_id=1, source_target_pairs={{0,16},{8,24},{16,0},{24,8},{1,17},{9,25},{17,1},{25,9},{2,18},{10... | collective-permute-start | bytes 76808 | tf_op jit(solution)/shard_map/ppermute | solution.py:230
  46.9 1.0 constant_dynamic-update-slice_fusion
  47.9 0.9 collective-permute-done.13
  48.8 0.9 collective-permute-start.14
  49.9 4.5 %collective-permute-start.2 = (bf16[160,2,256]{2,1,0:T(2,128)(2,1)S(1)}, bf16[160,2,256]{2,1,0:T(2,128)(2,1)S(1)}, u32[]{:S(2)}, u32[]{:S(2)}) collective-permute-start(bf16[160,2,256]{2,1,0:T(2,128)(2,1)S(1)} %get-tuple-element.44), channel_id=1, source_target_pairs={{0,8},{8,16},{16,24},{1,9},{9,17},{17,25},{2,10},{10,18},{18,26},{... | collective-permute-start | bytes 491528 | tf_op jit(solution)/shard_map/ppermute | solution.py:221
  54.4 1.9 %collective-permute-start.3 = (bf16[160,2,256]{2,1,0:T(2,128)(2,1)S(1)}, bf16[160,2,256]{2,1,0:T(2,128)(2,1)S(1)}, u32[]{:S(2)}, u32[]{:S(2)}) collective-permute-start(bf16[160,2,256]{2,1,0:T(2,128)(2,1)S(1)} %get-tuple-element.45), channel_id=1, source_target_pairs={{8,0},{16,8},{24,16},{9,1},{17,9},{25,17},{10,2},{18,10},{26,18},{... | collective-permute-start | bytes 491528 | tf_op jit(solution)/shard_map/ppermute | solution.py:221
  56.3 3.3 %collective-permute-start.1 = (bf16[80,64,128]{2,1,0:T(8,128)(2,1)}, bf16[80,64,128]{2,1,0:T(8,128)(2,1)S(1)}, u32[]{:S(2)}, u32[]{:S(2)}) collective-permute-start(bf16[80,64,128]{2,1,0:T(8,128)(2,1)} %get-tuple-element.25), channel_id=1, source_target_pairs={{1,0},{2,1},{3,2},{4,3},{5,4},{6,5},{7,6},{0,7},{9,8},{10,9},{11,1... | collective-permute-start | bytes 3932168 | tf_op jit(solution)/shard_map/ppermute | solution.py:221
  60.4 27.1 %collective-permute-done.15 = f32[80,80]{0,1:T(8,128)S(1)} collective-permute-done((f32[80,80]{0,1:T(8,128)S(1)}, f32[80,80]{0,1:T(8,128)S(1)}, u32[]{:S(2)}, u32[]{:S(2)}) %collective-permute-start.15) | collective-permute-done | bytes 25632 | tf_op jit(solution)/shard_map/ppermute | solution.py:230
  87.5 2.1 %collective-permute-start.16 = (f32[80,80]{0,1:T(8,128)S(1)}, f32[80,80]{0,1:T(8,128)S(1)}, u32[]{:S(2)}, u32[]{:S(2)}) collective-permute-start(f32[80,80]{0,1:T(8,128)S(1)} %add.61), channel_id=1, source_target_pairs={{0,4},{1,5},{2,6},{3,7},{4,0},{5,1},{6,2},{7,3},{8,12},{9,13},{10,... | collective-permute-start | bytes 76808 | tf_op jit(solution)/shard_map/ppermute | solution.py:230
  90.2 2.8 %setup.1 = (bf16[128,256]{1,0:T(8,128)(2,1)}, bf16[128,256]{1,0:T(8,128)(2,1)}, bf16[8,128]{1,0:T(8,128)(2,1)}, bf16[8,128]{1,0:T(8,128)(2,1)}, bf16[384,256]{1,...) custom-call(f32[8]{0:T(128)} %pad_maximum_fusion.2.refs_0_.taps_ref, ...), custom_call_target="tpu_custom_call" | custom-call | tf_op jit(solution)/shard_map/setup/pallas_call | solution.py:296
  93.1 7.3 %cholesky.20 = f32[80,80]{1,0:T(8,128)S(1)} custom-call(f32[80,80]{1,0:T(8,128)S(1)} %fusion.8), custom_call_target="Cholesky" | custom-call | tf_op jit(solution)/shard_map/jit(cholesky)/cholesky | solution.py:345
  101.3 1.3 select_bitcast_fusion
  104.3 21.6 %shard_map.205 = (f32[256,128]{1,0:T(8,128)}, bf16[80,64,128]{2,1,0:T(8,128)(2,1)}, bf16[80,64,128]{2,1,0:T(8,128)(2,1)}) custom-call(f32[8]{0:T(128)} %pad_maximum_fusion.2.refs_0_.taps_ref, bf16[80,256,128]{2,1,0:T(8,128)(2,1)} %bitcast.55, bf16[80,256,128]{2,1,0:T(8,128)(2,1)} %bitcast.51, bf16[640,256]{1,0:T(8,128)(2,1)} %get-tuple-element.42.ch_ref, ...), custom_call_target="tpu_custom_call" | custom-call | flops 10000000000 | bytes 20000000 | tf_op jit(solution)/shard_map/pallas_call | solution.py:321
  126.0 2.3 %multiply_reduce_fusion.1 = f32[64,128]{1,0:T(8,128)S(1)} fusion(bf16[80,64,128]{2,1,0:T(8,128)(2,1)} %get-tuple-element.34, bf16[80,64,128]{2,1,0:T(8,128)(2,1)S(1)} %collective-permute-done.1.er_ref), kind=kLoop, calls=%fused_computation.2 | loop fusion | flops 2613248 | bytes 2654208 | tf_op jit(solution)/shard_map/reduce_sum | solution.py:348
  128.3 4.1 %collective-permute-start.6 = (f32[64,128]{1,0:T(8,128)S(1)}, f32[64,128]{1,0:T(8,128)S(1)}, u32[]{:S(2)}, u32[]{:S(2)}) collective-permute-start(f32[64,128]{1,0:T(8,128)S(1)} %multiply_reduce_fusion.1), channel_id=1, source_target_pairs={{0,1},{1,2},{2,3},{3,4},{4,5},{5,6},{6,7},{7,0},{8,9},{9,10},{10,1... | collective-permute-start | bytes 98312 | tf_op jit(solution)/shard_map/ppermute | solution.py:221
  133.7 1.6 collective-permute-start.4
  135.3 2.8 %collective-permute-start.5 = (bf16[80,4,64]{2,1,0:T(4,128)(2,1)S(1)}, bf16[80,4,64]{2,1,0:T(4,128)(2,1)S(1)}, u32[]{:S(2)}, u32[]{:S(2)}) collective-permute-start(bf16[80,4,64]{2,1,0:T(4,128)(2,1)S(1)} %get-tuple-element.47), channel_id=1, source_target_pairs={{1,0},{2,1},{3,2},{4,3},{5,4},{6,5},{7,6},{0,7},{9,8},{10,9},{11,1... | collective-permute-start | bytes 122888 | tf_op jit(solution)/shard_map/ppermute | solution.py:221
  138.8 4.1 %shard_map.206 = (f32[256,128]{1,0:T(8,128)}, f32[8,256]{1,0:T(8,128)}) custom-call(f32[256,128]{1,0:T(8,128)} %fusion.7.inc_ref, s32[1,2048]{1,0:T(1,128)} %bitcast.64, f32[1,2048]{1,0:T(1,128)} %fusion.9.q_ref, f32[1,2048]{1,0:T(1,128)} %bitcast.68), custom_call_target="tpu_custom_call" | custom-call | tf_op jit(solution)/shard_map/pallas_call | solution.py:359
  143.7 5.2 %collective-permute-start.8 = (f32[2,256]{1,0:T(2,128)S(1)}, f32[2,256]{1,0:T(2,128)S(1)}, u32[]{:S(2)}, u32[]{:S(2)}) collective-permute-start(f32[2,256]{1,0:T(2,128)S(1)} %get-tuple-element.52), channel_id=1, source_target_pairs={{0,8},{8,16},{16,24},{1,9},{9,17},{17,25},{2,10},{10,18},{18,26},{... | collective-permute-start | bytes 6152 | tf_op jit(solution)/shard_map/ppermute | solution.py:221
  148.9 1.9 %collective-permute-start.9 = (f32[2,256]{1,0:T(2,128)S(1)}, f32[2,256]{1,0:T(2,128)S(1)}, u32[]{:S(2)}, u32[]{:S(2)}) collective-permute-start(f32[2,256]{1,0:T(2,128)S(1)} %get-tuple-element.53), channel_id=1, source_target_pairs={{8,0},{16,8},{24,16},{9,1},{17,9},{25,17},{10,2},{18,10},{26,18},{... | collective-permute-start | bytes 6152 | tf_op jit(solution)/shard_map/ppermute | solution.py:221
  150.8 1.0 fusion.13
  151.8 2.0 %collective-permute-done.9 = f32[2,256]{1,0:T(2,128)S(1)} collective-permute-done((f32[2,256]{1,0:T(2,128)S(1)}, f32[2,256]{1,0:T(2,128)S(1)}, u32[]{:S(2)}, u32[]{:S(2)}) %collective-permute-start.9) | collective-permute-done | bytes 2080 | tf_op jit(solution)/shard_map/ppermute | solution.py:221
  154.4 1.4 collective-permute-start.11
  156.4 1.0 maximum_bitcast_fusion.elat_ref
  158.0 3.7 %collective-permute-done.10 = f32[72,128]{1,0:T(8,128)S(1)} collective-permute-done((f32[72,128]{1,0:T(8,128)S(1)}, f32[72,128]{1,0:T(8,128)S(1)}, u32[]{:S(2)}, u32[]{:S(2)}) %collective-permute-start.10) | collective-permute-done | bytes 36896 | tf_op jit(solution)/shard_map/ppermute | solution.py:221
  163.0 20.3 %shard_map.207 = f32[80,256,128]{2,1,0:T(8,128)} custom-call(f32[8]{0:T(128)} %pad_maximum_fusion.2.refs_0_.taps_ref, bf16[80,256,128]{2,1,0:T(8,128)(2,1)} %bitcast.56, bf16[80,256,128]{2,1,0:T(8,128)(2,1)} %bitcast.52, bf16[80,64,128]{2,1,0:T(8,128)(2,1)} %copy-done.1, bf16[80,64,128]{2,1,0:T(8,128)(2,1)} %copy-done, ...), custom_call_target="tpu_custom_call" | custom-call | flops 10000000000 | bytes 24000000 | tf_op jit(solution)/shard_map/pallas_call | solution.py:381
  (76 shorter events, 10.8 us)
Async XLA Ops:
  2.0 10.6 %copy-start.7 = (s32[1,1,2048]{2,1,0:T(1,128)S(1)}, s32[1,1,2048]{2,1,0:T(1,128)}, u32[]{:S(2)}) copy-start(s32[1,1,2048]{2,1,0:T(1,128)} %param.25) | copy-start | bytes 24580
  12.6 10.1 %copy-start.5 = (f32[1,1,2048]{2,1,0:T(1,128)S(1)}, f32[1,1,2048]{2,1,0:T(1,128)}, u32[]{:S(2)}) copy-start(f32[1,1,2048]{2,1,0:T(1,128)} %param.29) | copy-start | bytes 24580
  25.1 18.9 %collective-permute-start.12 = (f32[80,80]{0,1:T(8,128)S(1)}, f32[80,80]{0,1:T(8,128)S(1)}, u32[]{:S(2)}, u32[]{:S(2)}) collective-permute-start(f32[80,80]{0,1:T(8,128)S(1)} %fusion.1), channel_id=1, source_target_pairs={{0,8},{8,0},{16,24},{24,16},{1,9},{9,1},{17,25},{25,17},{2,10},{10... | collective-permute-start | bytes 76808 | tf_op jit(solution)/shard_map/ppermute | solution.py:230
  43.0 16.8 %copy-start.6 = (s32[1,1,2048]{2,1,0:T(1,128)S(1)}, s32[1,1,2048]{2,1,0:T(1,128)}, u32[]{:S(2)}) copy-start(s32[1,1,2048]{2,1,0:T(1,128)} %param.27) | copy-start | bytes 24580
  43.0 46.6 %copy-start.8 = (f32[4]{0:T(128)S(1)}, f32[4]{0:T(128)}, u32[]{:S(2)}) copy-start(f32[4]{0:T(128)} %param.24) | copy-start | bytes 52
  43.0 46.6 %copy-start.9 = (f32[4]{0:T(128)S(1)}, f32[4]{0:T(128)}, u32[]{:S(2)}) copy-start(f32[4]{0:T(128)} %param.23) | copy-start | bytes 52
  44.1 4.7 %collective-permute-start.13 = (f32[80,80]{0,1:T(8,128)S(1)}, f32[80,80]{0,1:T(8,128)S(1)}, u32[]{:S(2)}, u32[]{:S(2)}) collective-permute-start(f32[80,80]{0,1:T(8,128)S(1)} %add.58), channel_id=1, source_target_pairs={{0,16},{8,24},{16,0},{24,8},{1,17},{9,25},{17,1},{25,9},{2,18},{10... | collective-permute-start | bytes 76808 | tf_op jit(solution)/shard_map/ppermute | solution.py:230
  48.8 10.9 %collective-permute-start.14 = (f32[80,80]{0,1:T(8,128)S(1)}, f32[80,80]{0,1:T(8,128)S(1)}, u32[]{:S(2)}, u32[]{:S(2)}) collective-permute-start(f32[80,80]{0,1:T(8,128)S(1)} %add.59), channel_id=1, source_target_pairs={{0,1},{1,0},{2,3},{3,2},{4,5},{5,4},{6,7},{7,6},{8,9},{9,8},{10,11... | collective-permute-start | bytes 76808 | tf_op jit(solution)/shard_map/ppermute | solution.py:230
  49.9 52.8 %collective-permute-start.2 = (bf16[160,2,256]{2,1,0:T(2,128)(2,1)S(1)}, bf16[160,2,256]{2,1,0:T(2,128)(2,1)S(1)}, u32[]{:S(2)}, u32[]{:S(2)}) collective-permute-start(bf16[160,2,256]{2,1,0:T(2,128)(2,1)S(1)} %get-tuple-element.44), channel_id=1, source_target_pairs={{0,8},{8,16},{16,24},{1,9},{9,17},{17,25},{2,10},{10,18},{18,26},{... | collective-permute-start | bytes 491528 | tf_op jit(solution)/shard_map/ppermute | solution.py:221
  54.4 48.2 %collective-permute-start.3 = (bf16[160,2,256]{2,1,0:T(2,128)(2,1)S(1)}, bf16[160,2,256]{2,1,0:T(2,128)(2,1)S(1)}, u32[]{:S(2)}, u32[]{:S(2)}) collective-permute-start(bf16[160,2,256]{2,1,0:T(2,128)(2,1)S(1)} %get-tuple-element.45), channel_id=1, source_target_pairs={{8,0},{16,8},{24,16},{9,1},{17,9},{25,17},{10,2},{18,10},{26,18},{... | collective-permute-start | bytes 491528 | tf_op jit(solution)/shard_map/ppermute | solution.py:221
  56.3 69.6 %collective-permute-start.1 = (bf16[80,64,128]{2,1,0:T(8,128)(2,1)}, bf16[80,64,128]{2,1,0:T(8,128)(2,1)S(1)}, u32[]{:S(2)}, u32[]{:S(2)}) collective-permute-start(bf16[80,64,128]{2,1,0:T(8,128)(2,1)} %get-tuple-element.25), channel_id=1, source_target_pairs={{1,0},{2,1},{3,2},{4,3},{5,4},{6,5},{7,6},{0,7},{9,8},{10,9},{11,1... | collective-permute-start | bytes 3932168 | tf_op jit(solution)/shard_map/ppermute | solution.py:221
  59.7 72.8 %collective-permute-start = (bf16[80,64,128]{2,1,0:T(8,128)(2,1)}, bf16[80,64,128]{2,1,0:T(8,128)(2,1)S(1)}, u32[]{:S(2)}, u32[]{:S(2)}) collective-permute-start(bf16[80,64,128]{2,1,0:T(8,128)(2,1)} %get-tuple-element.24), channel_id=1, source_target_pairs={{0,1},{1,2},{2,3},{3,4},{4,5},{5,6},{6,7},{7,0},{8,9},{9,10},{10,1... | collective-permute-start | bytes 3932168 | tf_op jit(solution)/shard_map/ppermute | solution.py:221
  59.7 27.8 %collective-permute-start.15 = (f32[80,80]{0,1:T(8,128)S(1)}, f32[80,80]{0,1:T(8,128)S(1)}, u32[]{:S(2)}, u32[]{:S(2)}) collective-permute-start(f32[80,80]{0,1:T(8,128)S(1)} %add.60), channel_id=1, source_target_pairs={{0,2},{1,3},{2,0},{3,1},{4,6},{5,7},{6,4},{7,5},{8,10},{9,11},{10,... | collective-permute-start | bytes 76808 | tf_op jit(solution)/shard_map/ppermute | solution.py:230
  87.5 5.5 %collective-permute-start.16 = (f32[80,80]{0,1:T(8,128)S(1)}, f32[80,80]{0,1:T(8,128)S(1)}, u32[]{:S(2)}, u32[]{:S(2)}) collective-permute-start(f32[80,80]{0,1:T(8,128)S(1)} %add.61), channel_id=1, source_target_pairs={{0,4},{1,5},{2,6},{3,7},{4,0},{5,1},{6,2},{7,3},{8,12},{9,13},{10,... | collective-permute-start | bytes 76808 | tf_op jit(solution)/shard_map/ppermute | solution.py:230
  93.1 11.0 %copy-start.3 = (bf16[128,256]{1,0:T(8,128)(2,1)S(1)}, bf16[128,256]{1,0:T(8,128)(2,1)}, u32[]{:S(2)}) copy-start(bf16[128,256]{1,0:T(8,128)(2,1)} %constant.69.clone.perm_ref) | copy-start | bytes 196612
  125.9 2.3 %copy-start = (bf16[80,64,128]{2,1,0:T(8,128)(2,1)}, bf16[80,64,128]{2,1,0:T(8,128)(2,1)S(1)}, u32[]{:S(2)}) copy-start(bf16[80,64,128]{2,1,0:T(8,128)(2,1)S(1)} %collective-permute-done.1.er_ref) | copy-start | bytes 3932164
  126.0 6.5 %copy-start.2 = (bf16[80,64,128]{2,1,0:T(8,128)(2,1)S(1)}, bf16[80,64,128]{2,1,0:T(8,128)(2,1)}, u32[]{:S(2)}) copy-start(bf16[80,64,128]{2,1,0:T(8,128)(2,1)} %get-tuple-element.35) | copy-start | bytes 3932164
  128.3 9.8 %collective-permute-start.6 = (f32[64,128]{1,0:T(8,128)S(1)}, f32[64,128]{1,0:T(8,128)S(1)}, u32[]{:S(2)}, u32[]{:S(2)}) collective-permute-start(f32[64,128]{1,0:T(8,128)S(1)} %multiply_reduce_fusion.1), channel_id=1, source_target_pairs={{0,1},{1,2},{2,3},{3,4},{4,5},{5,6},{6,7},{7,0},{8,9},{9,10},{10,1... | collective-permute-start | bytes 98312 | tf_op jit(solution)/shard_map/ppermute | solution.py:221
  132.4 1.1 copy-start.1
  132.4 5.7 %copy-start.4 = (f32[256,128]{1,0:T(8,128)S(1)}, f32[256,128]{1,0:T(8,128)}, u32[]{:S(2)}) copy-start(f32[256,128]{1,0:T(8,128)} %get-tuple-element.33) | copy-start | bytes 393220
  133.5 4.6 %collective-permute-start.7 = (f32[64,128]{1,0:T(8,128)S(1)}, f32[64,128]{1,0:T(8,128)S(1)}, u32[]{:S(2)}, u32[]{:S(2)}) collective-permute-start(f32[64,128]{1,0:T(8,128)S(1)} %multiply_reduce_fusion), channel_id=1, source_target_pairs={{1,0},{2,1},{3,2},{4,3},{5,4},{6,5},{7,6},{0,7},{9,8},{10,9},{11,1... | collective-permute-start | bytes 98312 | tf_op jit(solution)/shard_map/ppermute | solution.py:221
  133.7 22.6 %collective-permute-start.4 = (bf16[80,4,64]{2,1,0:T(4,128)(2,1)S(1)}, bf16[80,4,64]{2,1,0:T(4,128)(2,1)S(1)}, u32[]{:S(2)}, u32[]{:S(2)}) collective-permute-start(bf16[80,4,64]{2,1,0:T(4,128)(2,1)S(1)} %get-tuple-element.46), channel_id=1, source_target_pairs={{0,1},{1,2},{2,3},{3,4},{4,5},{5,6},{6,7},{7,0},{8,9},{9,10},{10,1... | collective-permute-start | bytes 122888 | tf_op jit(solution)/shard_map/ppermute | solution.py:221
  135.3 21.0 %collective-permute-start.5 = (bf16[80,4,64]{2,1,0:T(4,128)(2,1)S(1)}, bf16[80,4,64]{2,1,0:T(4,128)(2,1)S(1)}, u32[]{:S(2)}, u32[]{:S(2)}) collective-permute-start(bf16[80,4,64]{2,1,0:T(4,128)(2,1)S(1)} %get-tuple-element.47), channel_id=1, source_target_pairs={{1,0},{2,1},{3,2},{4,3},{5,4},{6,5},{7,6},{0,7},{9,8},{10,9},{11,1... | collective-permute-start | bytes 122888 | tf_op jit(solution)/shard_map/ppermute | solution.py:221
  143.7 8.1 %collective-permute-start.8 = (f32[2,256]{1,0:T(2,128)S(1)}, f32[2,256]{1,0:T(2,128)S(1)}, u32[]{:S(2)}, u32[]{:S(2)}) collective-permute-start(f32[2,256]{1,0:T(2,128)S(1)} %get-tuple-element.52), channel_id=1, source_target_pairs={{0,8},{8,16},{16,24},{1,9},{9,17},{17,25},{2,10},{10,18},{18,26},{... | collective-permute-start | bytes 6152 | tf_op jit(solution)/shard_map/ppermute | solution.py:221
  148.9 4.9 %collective-permute-start.9 = (f32[2,256]{1,0:T(2,128)S(1)}, f32[2,256]{1,0:T(2,128)S(1)}, u32[]{:S(2)}, u32[]{:S(2)}) collective-permute-start(f32[2,256]{1,0:T(2,128)S(1)} %get-tuple-element.53), channel_id=1, source_target_pairs={{8,0},{16,8},{24,16},{9,1},{17,9},{25,17},{10,2},{18,10},{26,18},{... | collective-permute-start | bytes 6152 | tf_op jit(solution)/shard_map/ppermute | solution.py:221
  154.4 3.0 %collective-permute-start.11 = (f32[72,128]{1,0:T(8,128)S(1)}, f32[72,128]{1,0:T(8,128)S(1)}, u32[]{:S(2)}, u32[]{:S(2)}) collective-permute-start(f32[72,128]{1,0:T(8,128)S(1)} %select_maximum_fusion), channel_id=1, source_target_pairs={{1,0},{2,1},{3,2},{4,3},{5,4},{6,5},{7,6},{0,7},{9,8},{10,9},{11,1... | collective-permute-start | bytes 110600 | tf_op jit(solution)/shard_map/ppermute | solution.py:221
  156.2 5.6 %collective-permute-start.10 = (f32[72,128]{1,0:T(8,128)S(1)}, f32[72,128]{1,0:T(8,128)S(1)}, u32[]{:S(2)}, u32[]{:S(2)}) collective-permute-start(f32[72,128]{1,0:T(8,128)S(1)} %select_maximum_fusion.1), channel_id=1, source_target_pairs={{0,1},{1,2},{2,3},{3,4},{4,5},{5,6},{6,7},{7,0},{8,9},{9,10},{10,1... | collective-permute-start | bytes 110600 | tf_op jit(solution)/shard_map/ppermute | solution.py:221
